TPU v7x, 128 devices: a whole 4x4x4 slice. The times are simulated.
128 devices in a mesh: row: 16 (over z, y), col: 8 (over x, core).
Axes of the slice: x: 4, y: 4, z: 4, core: 2. Of those that a mesh axis runs over, the one named last changes fastest.
Arguments:
- hidden: bfloat16 [4096, 8192], P('row', 'col'), may hold values from -96 to 96
- norm_gain: bfloat16 [8192], P('col'), may hold values from 0.5 to 1.5
- w_query: bfloat16 [8192, 4096], P('row', 'col')
- w_key: bfloat16 [8192, 4096], P('row', 'col')
- w_value: bfloat16 [8192, 4096], P('row', 'col'), may hold values from -0.0625 to 0.0625
- w_out: bfloat16 [4096, 8192], P('row', 'col'), may hold values from -0.09375 to 0.09375
Outputs:
- context: bfloat16 [4096, 4096], P('row', 'col')
- layer_out: bfloat16 [4096, 8192], P('row', 'col')
All inputs are finite; a program needn't handle non-finite values.
Results may differ from a plain program's by a relative error of at most 0.04.
Values may be sent and summed in bfloat16 or wider, within the bound.
A program may use at most 128 MiB of HBM per device.

v0:
```python
import math

import jax
import jax.numpy as jnp
from jax import lax
from jax.sharding import PartitionSpec as P

HD = 128


norm_epsilon = 1e-05


def rows_first(arrays, axis, dims):
    turned = [jnp.moveaxis(a, dim, 0) for a, dim in zip(arrays, dims)]
    widths = [t[0].size for t in turned]
    both = jnp.concatenate([t.reshape(-1, w) for t, w in zip(turned, widths)], axis=1)
    result = lax.all_gather(both, axis, axis=0, tiled=True)
    parts = jnp.split(result, [sum(widths[:k]) for k in range(1, len(widths))], axis=1)
    return tuple(
        (
            jnp.moveaxis(b.reshape(-1, *t.shape[1:]), 0, dim)
            for b, t, dim in zip(parts, turned, dims)
        )
    )


def side_by_side(arrays, axis, dim, along):
    widths = [a.shape[along] for a in arrays]
    both = jnp.concatenate(arrays, axis=along)
    result = lax.all_gather(both, axis, axis=dim, tiled=True)
    return tuple(jnp.split(result, [sum(widths[:k]) for k in range(1, len(widths))], axis=along))


def laid_out(parts, dim):
    parts = jnp.moveaxis(parts, 0, dim)
    lengths = parts.shape
    return parts.reshape(*lengths[:dim], lengths[dim] * lengths[dim + 1], *lengths[dim + 2 :])


def from_everyone(shard, axis):
    size = lax.axis_size(axis)
    return lax.all_to_all(
        jnp.broadcast_to(shard[None], (size, *shard.shape)), axis, 0, 0, tiled=True
    )


def gather_directly(shard, axis, dim):
    return laid_out(from_everyone(shard, axis), dim)


def rotary(values, positions):
    half = values.shape[-1] // 2
    freqs = jnp.exp(
        -math.log(10000.0) * 2.0 * jnp.arange(half, dtype=jnp.float32) / values.shape[-1]
    )
    angles = positions.astype(jnp.float32)[:, None] * freqs[None, :]
    cosine = jnp.cos(angles)[:, None, :]
    sine = jnp.sin(angles)[:, None, :]
    first = values[..., :half]
    second = values[..., half:]
    return jnp.concatenate(
        (first * cosine - second * sine, second * cosine + first * sine), axis=-1
    )


def blocked_sum(left, piece, block):
    count = piece.shape[0] // block
    split_left = left.reshape(left.shape[0], count, block)
    split_right = piece.reshape(count, block, piece.shape[1])
    terms = jnp.einsum("tbk,bkf->btf", split_left, split_right, preferred_element_type=jnp.float32)
    rounded = lax.optimization_barrier(terms.astype(jnp.bfloat16))
    return jnp.sum(rounded.astype(jnp.float32), axis=0)


def attend(carry, keys, values, queries, query_positions, key_positions, scale):
    peak, total, weighted = carry
    scores = jnp.einsum("qhd,khd->hqk", queries, keys, preferred_element_type=jnp.float32) * scale
    allowed = key_positions[None, :] <= query_positions[:, None]
    scores = jnp.where(allowed[None, :, :], scores, -jnp.inf)
    new_peak = jnp.maximum(peak, jnp.max(scores, axis=2))
    probs = jnp.exp(scores - new_peak[:, :, None])
    total = jnp.sum(probs, axis=2)
    weighted = jnp.einsum(
        "hqk,khd->hqd", probs.astype(jnp.bfloat16), values, preferred_element_type=jnp.float32
    )
    return (new_peak, total, weighted)


def start_state(heads_here, count):
    return (
        jnp.full((heads_here, count), -1e30, jnp.float32),
        jnp.zeros((heads_here, count), jnp.float32),
        jnp.zeros((heads_here, count, HD), jnp.float32),
    )


def finish(carry, count, heads_here):
    peak, total, weighted = carry
    return (
        (weighted / total[:, :, None])
        .transpose(1, 0, 2)
        .reshape(count, heads_here * HD)
        .astype(jnp.bfloat16)
    )


def on_device(hidden, norm_gain, w_query, w_key, w_value, w_out):
    rows = hidden.shape[0]
    residual = hidden.astype(jnp.float32)
    whole, gains = rows_first((hidden, norm_gain), "col", (1, 0))
    wide_rows = whole.astype(jnp.float32)
    mean_square = jnp.mean(wide_rows * wide_rows, axis=1, keepdims=True)
    normed = (
        wide_rows * lax.rsqrt(mean_square + norm_epsilon) * gains.astype(jnp.float32)[None, :]
    ).astype(jnp.bfloat16)
    block = w_query.shape[0]
    pieces = side_by_side((w_query, w_key, w_value), "row", 0, 1)
    segment = normed
    proj_q, proj_k, proj_v = tuple((blocked_sum(segment, piece, block) for piece in pieces))
    heads_here = w_query.shape[1] // HD
    row_index = lax.axis_index("row")
    first_row = row_index * rows
    positions = first_row + jnp.arange(rows, dtype=jnp.int32)
    query = rotary(proj_q.reshape(rows, heads_here, HD), positions).astype(jnp.bfloat16)
    keys_here = (
        rotary(proj_k.reshape(rows, heads_here, HD), positions)
        .astype(jnp.bfloat16)
        .reshape(rows, heads_here * HD)
    )
    values_here = proj_v.astype(jnp.bfloat16)
    scale = 1.0 / math.sqrt(HD)
    initial = start_state(heads_here, rows)
    pieces = side_by_side((keys_here, values_here), "row", 0, 1)
    keys = pieces[0].reshape(-1, heads_here, HD)
    values = pieces[1].reshape(-1, heads_here, HD)
    key_positions = jnp.arange(keys.shape[0], dtype=jnp.int32)
    folded = attend(initial, keys, values, query, positions, key_positions, scale)
    context = finish(folded, rows, heads_here)
    gathered_context = gather_directly(context, "col", 1)
    out_block = w_out.shape[0]
    segment = gathered_context
    attended = blocked_sum(segment, lax.all_gather(w_out, "row", axis=0, tiled=True), out_block)
    layer_out = (residual + attended).astype(jnp.bfloat16)
    return (context, layer_out)


def solution(mesh):
    placed = (
        P("row", "col"),
        P("col"),
        P("row", "col"),
        P("row", "col"),
        P("row", "col"),
        P("row", "col"),
    )
    return jax.shard_map(
        on_device,
        mesh=mesh,
        in_specs=placed,
        out_specs=(P("row", "col"), P("row", "col")),
        check_vma=False,
    )
```

profile of v0, /device:TPU:1, one launch (start us, length us, event | category | flops | bytes accessed | tf_op | source)
XLA Modules:
  0.0 393.5 jit_solution(4112995521757961650)
XLA Ops:
  7.2 0.0 all-gather.5.cloned.1.call-start
  7.2 0.7 reshape.144
  7.9 1.9 pad_maximum_fusion.1
  9.8 0.0 all-gather.5.cloned.1.call-update
  9.8 0.0 all-gather.7.cloned.1.call-start
  9.8 2.6 pad_maximum_fusion
  12.5 0.0 all-gather.9.cloned.1.call-start
  12.6 1.2 multiply_cosine_fusion
  13.8 32.3 %all-gather.5.cloned.1.call-done = bf16[8192,257]{0,1:T(8,128)(2,1)} async-done(((bf16[1024,257]{0,1:T(8,128)(2,1)}), bf16[8192,257]{0,1:T(8,128)(2,1)}) %all-gather.5.cloned.1.call-update) | async-done | bytes 4210704 | tf_op jit(solution)/shard_map/all_gather | solution.py:18
  46.1 3.1 fusion.3
  49.2 0.9 slice_convert_fusion
  50.1 5.4 %fusion.5 = bf16[8192,256]{0,1:T(8,128)(2,1)} fusion(f32[8192]{0:T(1024)S(1)} %bitcast.60, f32[256]{0:T(256)S(1)} %add_rsqrt_fusion, bf16[8192,257]{0,1:T(8,128)(2,1)} %all-gather.5.cloned.1.call-done), kind=kLoop, calls=%fused_computation.10 | loop fusion | flops 8388608 | bytes 8422400 | tf_op jit(solution)/shard_map/convert_element_type | solution.py:116
  55.6 146.4 %all-gather.7.cloned.1.call-done = bf16[8192,1536]{1,0:T(8,128)(2,1)} async-done(((bf16[512,1536]{1,0:T(8,128)(2,1)}), bf16[8192,1536]{1,0:T(8,128)(2,1)}) %all-gather.7.cloned.1.call-update) | async-done | bytes 25165840 | tf_op jit(solution)/shard_map/all_gather | solution.py:31
  201.9 12.4 %fusion.44 = (bf16[8192,512]{1,0:T(8,128)(2,1)S(1)}, bf16[8192,512]{1,0:T(8,128)(2,1)S(1)}, bf16[8192,512]{1,0:T(8,128)(2,1)}) fusion(bf16[8192,1536]{1,0:T(8,128)(2,1)} %all-gather.7.cloned.1.call-done), kind=kLoop, calls=%fused_computation.56 | loop fusion | bytes 50331648 | tf_op jit(solution)/shard_map/split | solution.py:32
  214.3 4.3 %fusion.24 = bf16[16,256,512]{2,1,0:T(8,128)(2,1)} fusion(bf16[16,512,512]{2,1,0:T(8,128)(2,1)S(1)} %bitcast.49, bf16[32,16,8,512]{3,2,1,0:T(8,128)(2,1)S(1)} %bitcast.51), kind=kOutput, calls=%fused_computation.28 | convolution fusion | flops 2149580800 | bytes 16777216 | tf_op jit(solution)/shard_map/tbk,bkf->btf/dot_general | solution.py:71
  218.6 2.3 fusion.18
  221.0 0.6 convert_reduce_fusion.2
  221.5 0.2 copy.25
  221.8 0.2 copy.43
  222.0 0.2 copy.42
  222.2 7.0 %fusion.21 = bf16[16,256,512]{2,1,0:T(8,128)(2,1)S(1)} fusion(bf16[16,512,512]{2,1,0:T(8,128)(2,1)} %bitcast.47, bf16[32,16,8,512]{3,2,1,0:T(8,128)(2,1)} %bitcast.50), kind=kOutput, calls=%fused_computation.27 | convolution fusion | flops 2149580800 | bytes 16777216 | tf_op jit(solution)/shard_map/tbk,bkf->btf/dot_general | solution.py:71
  229.2 0.6 convert_reduce_fusion.1
  229.8 0.2 copy.29
  230.1 0.2 copy.44
  230.3 0.2 copy.45
  230.5 0.3 subtract_convert_fusion.1
  230.8 0.1 pad_maximum_fusion.3
  230.9 0.1 copy.32
  231.1 0.1 copy.34
  231.2 2.8 reduce_sum.60
  234.1 0.9 pad_maximum_fusion.2
  235.0 0.0 all-gather.11.cloned.1.call-start
  235.0 0.5 all-gather.11.cloned.1.call-update
  235.6 0.7 iota_compare_fusion
  236.2 69.4 %all-gather.9.cloned.1.call-done = bf16[4096,1024]{1,0:T(8,128)(2,1)} async-done(((bf16[256,1024]{1,0:T(8,128)(2,1)}), bf16[4096,1024]{1,0:T(8,128)(2,1)}) %all-gather.9.cloned.1.call-update) | async-done | bytes 8388624 | tf_op jit(solution)/shard_map/all_gather | solution.py:31
  305.6 5.7 %fusion.45 = (bf16[4096,512]{1,0:T(8,128)(2,1)}, bf16[4096,512]{1,0:T(8,128)(2,1)}) fusion(bf16[4096,1024]{1,0:T(8,128)(2,1)} %all-gather.9.cloned.1.call-done), kind=kLoop, calls=%fused_computation.57 | loop fusion | bytes 16777216 | tf_op jit(solution)/shard_map/split | solution.py:32
  311.4 6.4 %copy.37 = bf16[4096,512]{0,1:T(8,128)(2,1)} copy(bf16[4096,512]{1,0:T(8,128)(2,1)} %get-tuple-element.12) | data formatting | bytes 8388608 | tf_op jit(solution)/shard_map/split | solution.py:32
  317.8 6.4 %copy.35 = bf16[4096,512]{0,1:T(8,128)(2,1)} copy(bf16[4096,512]{1,0:T(8,128)(2,1)} %get-tuple-element.11) | data formatting | bytes 8388608 | tf_op jit(solution)/shard_map/split | solution.py:32
  324.2 5.8 %fusion = (f32[4,256]{1,0:T(4,128)S(1)}, f32[4,256,4096]{2,1,0:T(8,128)S(1)}) fusion(pred[256,4096]{1,0:T(8,128)(4,1)S(1)} %iota_compare_fusion, bf16[4096,4,128]{0,2,1:T(8,128)(2,1)} %bitcast.44, bf16[256,4,64]{2,0,1:T(8,128)(2,1)S(1)} %get-tuple-element.14, bf16[256,4,64]{2,0,1:T(8,128)(2,1)S(1)} %get-tuple-element.13), kind=kOutput, calls=%fused_computation.3 | convolution fusion | flops 1086848000 | bytes 22286336 | tf_op jit(solution)/shard_map/qhd,khd->hqk/dot_general | solution.py:78
  330.0 4.4 %fusion.1 = f32[4,256]{1,0:T(4,128)S(1)} fusion(f32[4,256,4096]{2,1,0:T(8,128)S(1)} %get-tuple-element.26, f32[4,256]{1,0:T(4,128)S(1)} %broadcast_maximum_fusion, pred[256,4096]{1,0:T(8,128)(4,1)S(1)} %iota_compare_fusion), kind=kLoop, calls=%fused_computation.4 | loop fusion | flops 16776192 | bytes 17833984 | tf_op jit(solution)/shard_map/reduce_sum | solution.py:83
  334.5 6.7 %fusion.33 = bf16[256,4,128]{0,2,1:T(8,128)(2,1)S(1)} fusion(bf16[4096,4,128]{0,2,1:T(8,128)(2,1)} %bitcast.53, f32[4,256,4096]{2,1,0:T(8,128)S(1)} %get-tuple-element.26, f32[4,256]{1,0:T(4,128)S(1)} %broadcast_maximum_fusion, pred[256,4096]{1,0:T(8,128)(4,1)S(1)} %iota_compare_fusion, f32[256,4]{0,1:T(4,128)S(1)} %bitcast.61), kind=kOutput, calls=%fused_computation.33 | convolution fusion | flops 1090781184 | bytes 22290432 | tf_op jit(solution)/shard_map/hqk,khd->hqd/dot_general | solution.py:84
  341.1 1.5 broadcast_in_dim.15
  342.6 5.2 %all-to-all-start = ((bf16[8,256,512]{1,2,0:T(8,128)(2,1)}), bf16[8,256,512]{1,2,0:T(8,128)(2,1)S(1)}, u32[]{:S(2)}, u32[]{:S(2)}) async-start(bf16[8,256,512]{1,2,0:T(8,128)(2,1)} %broadcast_in_dim.15), calls=%async_computation | async-start | bytes 4194304 | tf_op jit(solution)/shard_map/all_to_all | solution.py:43
  347.8 0.8 copy.39
  348.7 29.5 %all-gather.11.cloned.1.call-done = bf16[4096,1024]{1,0:T(8,128)(2,1)} async-done(((bf16[256,1024]{1,0:T(8,128)(2,1)}), bf16[4096,1024]{1,0:T(8,128)(2,1)}) %all-gather.11.cloned.1.call-update) | async-done | bytes 8388624 | tf_op jit(solution)/shard_map/all_gather | solution.py:143
  378.2 5.8 %convolution_convert_fusion = bf16[16,256,1024]{2,1,0:T(8,128)(2,1)S(1)} fusion(bf16[256,16,256]{0,2,1:T(8,128)(2,1)S(1)} %bitcast.45, bf16[16,256,1024]{2,1,0:T(8,128)(2,1)} %bitcast.46), kind=kOutput, calls=%fused_computation.15 | convolution fusion | flops 2151677952 | bytes 18874368 | tf_op jit(solution)/shard_map/tbk,bkf->btf/dot_general | solution.py:71
  384.0 2.0 convert_reduce_fusion
  386.0 0.9 add_convert_fusion
  (17 shorter events, 0.2 us)
Async XLA Ops:
  7.2 38.9 %all-gather.5.cloned.1.call-start = ((), (), s32[]{:S(2)}) async-start(), calls=%async_computation.1 | async-start | bytes 4866048 | tf_op jit(solution)/shard_map/all_gather | solution.py:18
  9.8 192.1 %all-gather.7.cloned.1.call-start = ((), (), s32[]{:S(2)}) async-start(), calls=%async_computation.2 | async-start | bytes 26738688 | tf_op jit(solution)/shard_map/all_gather | solution.py:31
  12.5 293.2 %all-gather.9.cloned.1.call-start = ((), (), s32[]{:S(2)}) async-start(), calls=%async_computation.3 | async-start | bytes 8912896 | tf_op jit(solution)/shard_map/all_gather | solution.py:31
  201.9 12.4 %copy-start = (bf16[8192,256]{0,1:T(8,128)(2,1)S(1)}, bf16[8192,256]{0,1:T(8,128)(2,1)}, u32[]{:S(2)}) copy-start(bf16[8192,256]{0,1:T(8,128)(2,1)} %fusion.5) | copy-start | bytes 12582916
  229.2 1.3 copy-start.2
  229.2 1.3 copy-start.3
  235.0 143.2 %all-gather.11.cloned.1.call-start = ((), (), s32[]{:S(2)}) async-start(), calls=%async_computation.4 | async-start | bytes 8912896 | tf_op jit(solution)/shard_map/all_gather | solution.py:143
  342.6 35.5 %all-to-all-start = ((bf16[8,256,512]{1,2,0:T(8,128)(2,1)}), bf16[8,256,512]{1,2,0:T(8,128)(2,1)S(1)}, u32[]{:S(2)}, u32[]{:S(2)}) async-start(bf16[8,256,512]{1,2,0:T(8,128)(2,1)} %broadcast_in_dim.15), calls=%async_computation | async-start | bytes 4194304 | tf_op jit(solution)/shard_map/all_to_all | solution.py:43
  384.0 2.0 copy-start.1
Sparse Core Ops, SparseCore 0:
  9.9 36.1 all-gather.4
  48.2 153.6 all-gather.6
  235.1 70.5 all-gather.8
  307.6 70.5 all-gather.10
where the time goes:
time: 394 us; the launch traced here: 393 us
  waiting for transfers between devices  278 us (71%)
  local copies, waits for them, and re-layouts  35.5 us (9%)
  matrix products  31.9 us (8%)
  other arithmetic  28.6 us (7%)
  between operations  14 us (4%)
  starting transfers between devices  5.33 us (1%)
    all_gather x2, waiting for transfers between devices, side_by_side(): result = lax.all_gather(both, axis, axis=dim, tiled=True)  216 us
    all_gather x1, waiting for transfers between devices, rows_first(): result = lax.all_gather(both, axis, axis=0, tiled=True)  32.3 us
    split x4, local copies, waits for them, and re-layouts, side_by_side(): jnp.split(result, [sum(widths[:k]) for k in range(1, len(widths))], axis=...  31 us
    all_gather x1, waiting for transfers between devices, on_device(): lax.all_gather(w_out, 'row', axis=0, tiled=True)  29.5 us
    dot_general x4, matrix products, blocked_sum(): jnp.einsum('tbk,bkf->btf', split_left, split_right, preferred_element_typ...  19.4 us
  transfers between devices with their start and end apart: 5, of which 4 were waited for; matrix products, arithmetic and copies ran while one was open for 13% of the time, Pallas kernels for 0%

commit v1 on v0

v1 whole, which is shorter than its diff:
```python
import math

import jax
import jax.numpy as jnp
import numpy as np
from jax import lax
from jax.experimental import pallas as pl
from jax.experimental.pallas import tpu as pltpu
from jax.sharding import Mesh, PartitionSpec as P

HD = 128
EPS = 1e-5
MESH = pl.DeviceIdType.MESH
BF = jnp.bfloat16
F32 = jnp.float32


def rotary_tables(block, blocks):
    freqs = np.exp(-math.log(10000.0) * 2.0 * np.arange(HD // 2) / HD)
    freqs = np.concatenate([freqs, freqs])[None, :]
    base = (np.arange(blocks) * block)[:, None] * freqs
    rows = np.arange(block)[:, None] * freqs
    angles = np.concatenate([base, rows], axis=0)
    return np.concatenate([np.cos(angles), np.sin(angles)], axis=1).astype(np.float32)


class Ids:
    def __init__(self):
        self.table = {}

    def __call__(self, *name):
        return self.table.setdefault(name, len(self.table))


N_MESSAGES = 160


def kernel(
    features, hidden, gain, wq, wk, wv, wout, tables,
    ctx_out, layer_out,
    xg, gbuf, xs, ssq, sqs, rsc, wg, pbuf, tr, fin, kvg, qbuf, sbuf,
    cown, ctxs, cx, wog, op, otr, ofin, send_sem, recv_sem, local_sem,
):
    z, y, x, c = (lax.axis_index(n) for n in ("z", "y", "x", "c"))
    zr, zl, zf = (lax.rem(z + k, 4) for k in (1, 3, 2))
    yr, yl, yf = (lax.rem(y + k, 4) for k in (1, 3, 2))
    xr, xl, xf = (lax.rem(x + k, 4) for k in (1, 3, 2))
    other = 1 - c
    block = hidden.shape[0]
    half = block // 2
    ids = Ids()
    sends = []

    def message(src, dst, name, **where):
        i = ids(*name)
        return pltpu.make_async_remote_copy(
            src_ref=src, dst_ref=dst, send_sem=send_sem.at[i], recv_sem=recv_sem.at[i],
            device_id=where, device_id_type=MESH,
        )

    def send(src, dst, name, **where):
        copy = message(src, dst, name, **where)
        copy.start()
        sends.append(copy)

    def arrived(dst, name, **where):
        message(dst, dst, name, **where).wait_recv()

    barrier = pltpu.get_barrier_semaphore()
    partners = [{"z": zr}, {"z": zl}, {"z": zf}, {"y": yr}, {"y": yl}, {"x": xr}, {"x": xl}, {"c": other}]
    for where in partners:
        pl.semaphore_signal(barrier, inc=1, device_id=where, device_id_type=MESH)

    @pl.when(x != z)
    def _():
        pl.semaphore_signal(barrier, inc=1, device_id={"z": x, "x": z}, device_id_type=MESH)

    pl.semaphore_wait(barrier, len(partners) + jnp.where(x != z, 1, 0))

    def swap_start(src, dst, name):
        copy = message(src, dst, name, z=x, x=z)
        local = pltpu.make_async_copy(src, dst, local_sem.at[ids(*name)])

        @pl.when(x != z)
        def _():
            copy.start()

        @pl.when(x == z)
        def _():
            local.start()

    def swap_arrived(src, dst, name):
        copy = message(src, dst, name, z=x, x=z)
        local = pltpu.make_async_copy(src, dst, local_sem.at[ids(*name)])

        @pl.when(x != z)
        def _():
            copy.wait_recv()
            copy.wait_send()

        @pl.when(x == z)
        def _():
            local.wait()

    def gather_y(slot, name):
        send(slot(y, None), slot(y, None), (name, "r"), y=yr)
        send(slot(y, None), slot(y, None), (name, "l"), y=yl)

    def forward_y(slot, name):
        arrived(slot(yl, None), (name, "r"), y=yr)
        send(slot(yl, 0), slot(yl, 0), (name, "fr"), y=yr)
        arrived(slot(yr, None), (name, "l"), y=yl)
        send(slot(yr, 1), slot(yr, 1), (name, "fl"), y=yl)

    def finish_y(slot, name):
        arrived(slot(yf, 0), (name, "fr"), y=yr)
        arrived(slot(yf, 1), (name, "fl"), y=yl)

    weights = {"k": wk, "v": wv, "q": wq}
    order = {"k": 0, "v": 1, "q": 2}
    wrows = wk.shape[0]

    def weight_slot(name):
        def slot(owner, part):
            ref = wg.at[order[name], owner]
            return ref if part is None else ref.at[pl.ds(part * (wrows // 2), wrows // 2)]
        return slot

    def weight_gather(name):
        mine = weights[name]
        dst = weight_slot(name)(y, None)
        send(mine, dst, ("w" + name, "r"), y=yr)
        send(mine, dst, ("w" + name, "l"), y=yl)

    def rows(ref, h):
        return ref.at[pl.ds(h * half, half)]

    def x_slot(plane, t, h):
        return rows(xg.at[plane, t], h)

    weight_gather("k")
    for h in range(2):
        swap_start(rows(hidden, h), x_slot(c, z, h), ("xp", h))
    swap_start(gain, gbuf.at[c], ("gp",))
    weight_gather("v")
    local_w = []
    for name in "kvq":
        copy = pltpu.make_async_copy(weights[name], wg.at[order[name], y], local_sem.at[ids("lw", name)])
        copy.start()
        local_w.append(copy)

    def process(plane, t, first):
        g = gbuf[plane].astype(F32)
        width = g.shape[1]

        @pl.loop(0, block // 32)
        def _(i):
            r = pl.ds(pl.multiple_of(i * 32, 32), 32)
            v = xg[plane, t, r, :].astype(F32)
            xs[plane, t, r, :] = (v * g).astype(BF)
            sq = v * v
            total = sq[:, :HD]
            for k in range(1, width // HD):
                total = total + sq[:, k * HD:(k + 1) * HD]
            if first:
                ssq[t, r, :] = total
            else:
                ssq[t, r, :] = ssq[t, r, :] + total

    def pair_send(t, label, h):
        send(x_slot(c, t, h), x_slot(c, t, h), ("pair", label, h), c=other)

    swap_arrived(gain, gbuf.at[c], ("gp",))
    send(gbuf.at[c], gbuf.at[c], ("gpair",), c=other)
    for h in range(2):
        swap_arrived(rows(hidden, h), x_slot(c, x, h), ("xp", h))
        send(x_slot(c, x, h), x_slot(c, x, h), ("xr", h), x=xr)
        send(x_slot(c, x, h), x_slot(c, x, h), ("xl", h), x=xl)
        pair_send(x, "own", h)
    forward_y(weight_slot("k"), "wk")
    process(c, x, True)
    arrived(x_slot(c, xl, 0), ("xr", 0), x=xr)
    send(x_slot(c, xl, 0), x_slot(c, xl, 0), ("xfr",), x=xr)
    pair_send(xl, "left", 0)
    arrived(x_slot(c, xr, 0), ("xl", 0), x=xl)
    pair_send(xr, "right", 0)
    forward_y(weight_slot("v"), "wv")
    weight_gather("q")
    arrived(x_slot(c, xr, 1), ("xl", 1), x=xl)
    send(x_slot(c, xr, 1), x_slot(c, xr, 1), ("xfl",), x=xl)
    pair_send(xr, "right", 1)
    arrived(x_slot(c, xl, 1), ("xr", 1), x=xr)
    pair_send(xl, "left", 1)
    arrived(gbuf.at[other], ("gpair",), c=other)
    process(c, xr, True)
    process(c, xl, True)
    for h in range(2):
        arrived(x_slot(other, x, h), ("pair", "own", h), c=other)
    process(other, x, False)
    arrived(x_slot(c, xf, 0), ("xfr",), x=xr)
    pair_send(xf, "far", 0)
    arrived(x_slot(c, xf, 1), ("xfl",), x=xl)
    pair_send(xf, "far", 1)
    process(c, xf, True)
    for t, label in ((xr, "right"), (xl, "left"), (xf, "far")):
        for h in range(2):
            arrived(x_slot(other, t, h), ("pair", label, h), c=other)
        process(other, t, False)
    for t in range(4):
        s = jnp.sum(ssq[t].T, axis=0, keepdims=True)
        sqs[z, t] = jnp.broadcast_to(s, (8, block))
    for where, label in ((zr, 1), (zl, 3), (zf, 2)):
        send(sqs.at[z], sqs.at[z], ("sq", label), z=where)

    cw = wk.shape[1]

    def lower(ref):
        return ref.at[pl.ds(0, 2 * block)]

    def upper(ref):
        return ref.at[pl.ds(2 * block, 2 * block)]

    def project(name):
        j = order[name]
        width = xs.shape[3]
        tokens = 4 * block

        @pl.loop(0, cw // 256)
        def _(n):
            cols = pl.ds(pl.multiple_of(n * 256, 256), 256)
            w0 = wg[j, 0:2, :, cols].reshape(width, 256)
            w1 = wg[j, 2:4, :, cols].reshape(width, 256)
            left0 = xs[0].reshape(tokens, width)
            left1 = xs[1].reshape(tokens, width)
            acc = jnp.dot(left0, w0, preferred_element_type=F32)
            acc = acc + jnp.dot(left1, w1, preferred_element_type=F32)
            pbuf[j, 2 * n] = acc[:, :HD].astype(BF)
            pbuf[j, 2 * n + 1] = acc[:, HD:].astype(BF)

        send(lower(pbuf.at[j, zf]), tr.at[j, 0], (name, "ta"), z=zr)
        send(upper(pbuf.at[j, zf]), tr.at[j, 1], (name, "tb"), z=zl)
        send(upper(pbuf.at[j, zr]), upper(fin.at[j, 0]), (name, "a1"), z=zr)
        send(lower(pbuf.at[j, zl]), lower(fin.at[j, 1]), (name, "b0"), z=zl)

    def relay(name):
        j = order[name]
        lo, hi = pl.ds(0, 2 * block), pl.ds(2 * block, 2 * block)
        arrived(tr.at[j, 0], (name, "ta"), z=zr)
        pbuf[j, zr, lo, :] = (pbuf[j, zr, lo, :].astype(F32) + tr[j, 0].astype(F32)).astype(BF)
        send(lower(pbuf.at[j, zr]), lower(fin.at[j, 0]), (name, "a0"), z=zr)
        arrived(tr.at[j, 1], (name, "tb"), z=zl)
        pbuf[j, zl, hi, :] = (pbuf[j, zl, hi, :].astype(F32) + tr[j, 1].astype(F32)).astype(BF)
        send(upper(pbuf.at[j, zl]), upper(fin.at[j, 1]), (name, "b1"), z=zl)

    def reduced(name):
        j = order[name]
        arrived(upper(fin.at[j, 0]), (name, "a1"), z=zr)
        arrived(lower(fin.at[j, 1]), (name, "b0"), z=zl)
        arrived(lower(fin.at[j, 0]), (name, "a0"), z=zr)
        arrived(upper(fin.at[j, 1]), (name, "b1"), z=zl)

    def total_of(name, t):
        j = order[name]
        r = pl.ds(t * block, block)
        total = pbuf[j, z, r, :].astype(F32) + fin[j, 0, r, :].astype(F32) + fin[j, 1, r, :].astype(F32)
        return total * rsc[r, :]

    def rotated(v, t):
        bases = tables[:16, :]
        here = lax.broadcasted_iota(jnp.int32, bases.shape, 0) == 4 * t + y
        base = jnp.sum(jnp.where(here, bases, 0.0), axis=0, keepdims=True)
        ca, sa = base[:, :HD], base[:, HD:]
        ci, si = tables[16:, :HD], tables[16:, HD:]
        cos = ca * ci - sa * si
        sin = sa * ci + ca * si
        lane = lax.broadcasted_iota(jnp.int32, (block, HD), 1)
        signed = jnp.where(lane < HD // 2, -sin, sin)
        return v * cos + pltpu.roll(v, HD // 2, axis=1) * signed

    for copy in local_w:
        copy.wait()
    finish_y(weight_slot("k"), "wk")
    project("k")
    finish_y(weight_slot("v"), "wv")
    project("v")
    forward_y(weight_slot("q"), "wq")
    relay("k")

    for where, label in ((zr, 1), (zl, 3), (zf, 2)):
        src = {1: zl, 3: zr, 2: zf}[label]
        arrived(sqs.at[src], ("sq", label), z=where)
    for t in range(4):
        s = sqs[0, t] + sqs[1, t] + sqs[2, t] + sqs[3, t]
        factor = lax.rsqrt(s / features + EPS)
        rsc[pl.ds(t * block, block), :] = jnp.broadcast_to(factor[0:1, :], (HD, block)).T

    def kv_slot(which):
        def slot(owner, part):
            ref = kvg.at[which]
            return ref.at[:, owner] if part is None else ref.at[pl.ds(2 * part, 2), owner]
        return slot

    def out_slot(owner, part):
        ref = wog.at[owner]
        count = wout.shape[0] // 2
        return ref if part is None else ref.at[pl.ds(part * count, count)]

    relay("v")
    reduced("k")
    for t in range(4):
        kvg[0, t, y] = rotated(total_of("k", t), t).astype(BF)
    gather_y(kv_slot(0), "k")
    finish_y(weight_slot("q"), "wq")
    project("q")
    reduced("v")
    for t in range(4):
        kvg[1, t, y] = total_of("v", t).astype(BF)
    gather_y(kv_slot(1), "v")
    relay("q")
    forward_y(kv_slot(0), "k")
    forward_y(kv_slot(1), "v")
    send(wout, wog.at[y], ("wo", "r"), y=yr)
    send(wout, wog.at[y], ("wo", "l"), y=yl)
    wo_copy = pltpu.make_async_copy(wout, wog.at[y], local_sem.at[ids("lwo")])
    wo_copy.start()
    reduced("q")
    for t in range(4):
        qbuf[t] = rotated(total_of("q", t), t).astype(BF)
    finish_y(kv_slot(0), "k")
    finish_y(kv_slot(1), "v")

    factor = math.log2(math.e) / math.sqrt(HD)
    span = 4 * block

    def keys(which, kb):
        return kvg[which, kb].reshape(span, HD)

    def cx_slot(plane, owner, t):
        return cx.at[plane, owner, pl.ds(t * block, block)]

    heads_base = [ids("c2", k) for k in range(4)][0]

    def head_copy(src, dst, target, source):
        return pltpu.make_async_remote_copy(
            src_ref=src, dst_ref=dst, send_sem=send_sem.at[heads_base + target],
            recv_sem=recv_sem.at[heads_base + source], device_id={"z": target}, device_id_type=MESH,
        )

    def context_sends(t):
        mine = cown.at[pl.ds(t * block, block)]

        @pl.when(z != t)
        def _():
            head_copy(mine, ctxs.at[z], t, z).start()

        @pl.when(z == t)
        def _():
            ctxs[z] = cown[pl.ds(t * block, block), :]

        swap_start(mine, cx_slot(c, z, t), ("cp", t))

    for t in range(4):
        q = qbuf[t]

        def score(kb, peak):
            s = lax.dot_general(q, keys(0, kb), (((1,), (1,)), ((), ())), preferred_element_type=F32)
            sbuf[kb] = s
            return jnp.maximum(peak, jnp.max(s, axis=1, keepdims=True))

        peak = jnp.full((block, 1), -1e30, F32)
        if t > 0:
            peak = lax.fori_loop(0, t, score, peak)
        s = lax.dot_general(q, keys(0, t), (((1,), (1,)), ((), ())), preferred_element_type=F32)
        row = lax.broadcasted_iota(jnp.int32, (block, span), 0) + y * block
        col = lax.broadcasted_iota(jnp.int32, (block, span), 1)
        s = jnp.where(col <= row, s, -jnp.inf)
        sbuf[t] = s
        peak = jnp.maximum(peak, jnp.max(s, axis=1, keepdims=True))

        def weigh(kb, carry):
            total, acc = carry
            p = jnp.exp2((sbuf[kb] - peak) * factor)
            total = total + jnp.sum(p, axis=1, keepdims=True)
            acc = acc + jnp.dot(p.astype(BF), keys(1, kb), preferred_element_type=F32)
            return total, acc

        total, acc = lax.fori_loop(
            0, t + 1, weigh, (jnp.zeros((block, 1), F32), jnp.zeros((block, HD), F32))
        )
        cown[pl.ds(t * block, block), :] = (acc / total).astype(BF)
        context_sends(t)
        if t == 1:
            forward_y(out_slot, "wo")

    def cx_part(plane, owner, h):
        return cx.at[plane, owner, pl.ds(2 * h * block, 2 * block)]

    for h in range(2):
        for t in (2 * h, 2 * h + 1):
            mine = cown.at[pl.ds(t * block, block)]
            swap_arrived(mine, cx_slot(c, x, t), ("cp", t))
        send(cx_part(c, x, h), cx_part(c, x, h), ("cr", h), x=xr)
        send(cx_part(c, x, h), cx_part(c, x, h), ("cl", h), x=xl)
        send(cx_part(c, x, h), cx_part(c, x, h), ("cpair", "own", h), c=other)

    def cx_pair(owner, label, h):
        send(cx_part(c, owner, h), cx_part(c, owner, h), ("cpair", label, h), c=other)

    arrived(cx_part(c, xl, 0), ("cr", 0), x=xr)
    send(cx_part(c, xl, 0), cx_part(c, xl, 0), ("cfr",), x=xr)
    cx_pair(xl, "left", 0)
    arrived(cx_part(c, xr, 0), ("cl", 0), x=xl)
    cx_pair(xr, "right", 0)
    arrived(cx_part(c, xr, 1), ("cl", 1), x=xl)
    send(cx_part(c, xr, 1), cx_part(c, xr, 1), ("cfl",), x=xl)
    cx_pair(xr, "right", 1)
    arrived(cx_part(c, xl, 1), ("cr", 1), x=xr)
    cx_pair(xl, "left", 1)

    for h in range(4):
        @pl.when(z != h)
        def _():
            copy = head_copy(cown.at[pl.ds(h * block, block)], ctxs.at[h], h, h)
            copy.wait_send()
            copy.wait_recv()

    for h in range(4):
        ctx_out[:, h * HD:(h + 1) * HD] = ctxs[h]

    wo_copy.wait()
    finish_y(out_slot, "wo")
    arrived(cx_part(c, xf, 0), ("cfr",), x=xr)
    cx_pair(xf, "far", 0)
    arrived(cx_part(c, xf, 1), ("cfl",), x=xl)
    cx_pair(xf, "far", 1)
    for label, owner in (("own", x), ("left", xl), ("right", xr), ("far", xf)):
        for h in range(2):
            arrived(cx_part(other, owner, h), ("cpair", label, h), c=other)

    def out_product(d):
        r = pl.ds(pl.multiple_of(d * block, block), block)
        left = jnp.concatenate([cx[p, k, r, :] for p in range(2) for k in range(4)], axis=1)
        right = wog[...].reshape(left.shape[1], wog.shape[2])
        return jnp.dot(left, right, preferred_element_type=F32)

    def first(ref):
        return ref.at[pl.ds(0, half)]

    def second(ref):
        return ref.at[pl.ds(half, half)]

    op[zf] = out_product(zf).astype(BF)
    send(first(op.at[zf]), otr.at[0], ("o", "ta"), z=zr)
    send(second(op.at[zf]), otr.at[1], ("o", "tb"), z=zl)
    op[zr] = out_product(zr).astype(BF)
    send(second(op.at[zr]), second(ofin.at[0]), ("o", "a1"), z=zr)
    op[zl] = out_product(zl).astype(BF)
    send(first(op.at[zl]), first(ofin.at[1]), ("o", "b0"), z=zl)
    lo, hi = pl.ds(0, half), pl.ds(half, half)
    arrived(otr.at[0], ("o", "ta"), z=zr)
    op[zr, lo, :] = (op[zr, lo, :].astype(F32) + otr[0].astype(F32)).astype(BF)
    send(first(op.at[zr]), first(ofin.at[0]), ("o", "a0"), z=zr)
    arrived(otr.at[1], ("o", "tb"), z=zl)
    op[zl, hi, :] = (op[zl, hi, :].astype(F32) + otr[1].astype(F32)).astype(BF)
    send(second(op.at[zl]), second(ofin.at[1]), ("o", "b1"), z=zl)
    oacc = hidden[...].astype(F32) + out_product(z)
    arrived(second(ofin.at[0]), ("o", "a1"), z=zr)
    arrived(first(ofin.at[1]), ("o", "b0"), z=zl)
    arrived(first(ofin.at[0]), ("o", "a0"), z=zr)
    arrived(second(ofin.at[1]), ("o", "b1"), z=zl)
    layer_out[...] = (oacc + ofin[0].astype(F32) + ofin[1].astype(F32)).astype(BF)
    for copy in sends:
        copy.wait_send()


def on_device(hidden, norm_gain, w_query, w_key, w_value, w_out):
    block, width = hidden.shape
    wrows, cw = w_query.shape
    orows, ow = w_out.shape
    features = 8 * width
    tables = jnp.asarray(rotary_tables(block, 16))
    vmem = pl.BlockSpec(memory_space=pltpu.VMEM)

    def body(*refs):
        kernel(features, *refs)

    return pl.pallas_call(
        body,
        out_shape=(
            jax.ShapeDtypeStruct((block, cw), BF),
            jax.ShapeDtypeStruct((block, ow), BF),
        ),
        in_specs=[vmem] * 7,
        out_specs=(vmem, vmem),
        scratch_shapes=[
            pltpu.VMEM((2, 4, block, width), BF),
            pltpu.VMEM((2, 1, width), BF),
            pltpu.VMEM((2, 4, block, width), BF),
            pltpu.VMEM((4, block, HD), F32),
            pltpu.VMEM((4, 4, 8, block), F32),
            pltpu.VMEM((4 * block, HD), F32),
            pltpu.VMEM((3, 4, wrows, cw), BF),
            pltpu.VMEM((3, 4, 4 * block, HD), BF),
            pltpu.VMEM((3, 2, 2 * block, HD), BF),
            pltpu.VMEM((3, 2, 4 * block, HD), BF),
            pltpu.VMEM((2, 4, 4, block, HD), BF),
            pltpu.VMEM((4, block, HD), BF),
            pltpu.VMEM((4, block, 4 * block), F32),
            pltpu.VMEM((4 * block, HD), BF),
            pltpu.VMEM((4, block, HD), BF),
            pltpu.VMEM((2, 4, 4 * block, HD), BF),
            pltpu.VMEM((4, orows, ow), BF),
            pltpu.VMEM((4, block, ow), BF),
            pltpu.VMEM((2, block // 2, ow), BF),
            pltpu.VMEM((2, block, ow), BF),
            pltpu.SemaphoreType.DMA((N_MESSAGES,)),
            pltpu.SemaphoreType.DMA((N_MESSAGES,)),
            pltpu.SemaphoreType.DMA((N_MESSAGES,)),
        ],
        compiler_params=pltpu.CompilerParams(
            collective_id=0, has_side_effects=True, vmem_limit_bytes=62 * 1024 * 1024
        ),
    )(hidden, norm_gain.reshape(1, width), w_query, w_key, w_value, w_out, tables)


def solution(mesh):
    cube = Mesh(mesh.devices.reshape(4, 4, 4, 2), ("z", "y", "x", "c"))
    rows, cols = ("z", "y"), ("x", "c")
    both = P(rows, cols)
    return jax.shard_map(
        on_device,
        mesh=cube,
        in_specs=(both, P(cols), both, both, both, both),
        out_specs=(both, both),
        check_vma=False,
    )
```

time: 394 us -> 156 us (0.40)
  waiting for transfers between devices: 278 us -> 0 us
  Pallas kernels: 0 us -> 150 us
  matrix products: 31.9 us -> 0 us
  local copies, waits for them, and re-layouts: 35.5 us -> 3.8 us
  other arithmetic: 28.6 us -> 0 us
  between operations: 14 us -> 0.65 us
  starting transfers between devices: 5.33 us -> 0 us
    all_gather x4 -> x0, waiting for transfers between devices: 278 us -> none  [the longest x2 216 us: side_by_side(): result = lax.all_gather(both, axis, axis=dim, tiled=True)]
    pallas_call x0 -> x1, Pallas kernels: none -> 150 us  [on_device(): pl.pallas_call(body, out_shape=(jax.ShapeDtypeStruct((block, cw), BF), ja...]
    dot_general x6 -> x0, matrix products: 31.9 us -> none  [the longest x4 19.4 us: blocked_sum(): jnp.einsum('tbk,bkf->btf', split_left, split_right, preferred_element_typ...]
    split x4 -> x0, local copies, waits for them, and re-layouts: 31 us -> none  [side_by_side(): jnp.split(result, [sum(widths[:k]) for k in range(1, len(widths))], axis=...]
    reduce_sum x6 -> x0, other arithmetic: 13.6 us -> none  [the longest x4 6.02 us: blocked_sum(): return jnp.sum(rounded.astype(jnp.float32), axis=0)]
    convert_element_type x3 -> x0, other arithmetic: 7.28 us -> none  [the longest x1 5.41 us: on_device(): normed = (wide_rows * lax.rsqrt(mean_square + norm_epsilon) * gains.astyp...]
    concatenate x4 -> x0, other arithmetic: 5.51 us -> none  [the longest x2 3.49 us: side_by_side(): both = jnp.concatenate(arrays, axis=along)]
    all_to_all x1 -> x0, starting transfers between devices: 5.17 us -> none  [from_everyone(): lax.all_to_all(jnp.broadcast_to(shard[None], (size, *shard.shape)), axis,...]
  transfers between devices with their start and end apart: 5 -> 0, of which waited for: 4 -> 0; matrix products, arithmetic and copies ran while one was open for 13% -> 0% of each run, Pallas kernels for 0% -> 0%
where the time goes in v1:
time: 156 us; the launch traced here: 155 us
  Pallas kernels  150 us (96%)
  local copies, waits for them, and re-layouts  3.8 us (2%)
    pallas_call x1, Pallas kernels, on_device(): pl.pallas_call(body, out_shape=(jax.ShapeDtypeStruct((block, cw), BF), ja...  150 us

profile of v1, /device:TPU:1, one launch (start us, length us, event | category | flops | bytes accessed | tf_op | source)
XLA Modules:
  0.0 154.6 jit_solution(10808179566900331567)
XLA Ops:
  0.6 1.3 reshape.7.refs_1_
  1.9 150.1 %shard_map.86 = (bf16[256,512]{1,0:T(8,128)(2,1)}, bf16[256,1024]{1,0:T(8,128)(2,1)}) custom-call(bf16[256,1024]{1,0:T(8,128)(2,1)} %refs_0_.1, bf16[1,1024]{1,0:T(2,128)(2,1)} %reshape.7.refs_1_, bf16[512,512]{1,0:T(8,128)(2,1)} %refs_2_.1, bf16[512,512]{1,0:T(8,128)(2,1)} %refs_3_.1, bf16[512,512]{1,0:T(8,128)(2,1)} %refs_4_.1, bf16[256,1024]{1,0:T(8,128)(2,1)} %refs_5_.1, ...), custom_call_target="tpu_custom_call" | custom-call | tf_op jit(solution)/shard_map/pallas_call | solution.py:487
  152.0 0.0 copy-start
  152.0 1.7 %copy.11 = bf16[256,512]{1,0:T(8,128)(2,1)} copy(bf16[256,512]{1,0:T(8,128)(2,1)} %get-tuple-element.4) | data formatting | bytes 524288
  153.8 0.0 copy-done
  153.8 0.8 copy.12
Async XLA Ops:
  152.0 1.7 %copy-start = (bf16[256,1024]{1,0:T(8,128)(2,1)S(1)}, bf16[256,1024]{1,0:T(8,128)(2,1)}, u32[]{:S(2)}) copy-start(bf16[256,1024]{1,0:T(8,128)(2,1)} %get-tuple-element.5) | copy-start | bytes 1572868

commit v2 on v1

--- a/solution.py
+++ b/solution.py
@@ -36,10 +36,10 @@
 
 
 def kernel(
-    features, hidden, gain, wq, wk, wv, wout, tables,
+    features, hidden, wq, wk, wv, wout, gain, tables,
     ctx_out, layer_out,
-    xg, gbuf, xs, ssq, sqs, rsc, wg, pbuf, tr, fin, kvg, qbuf, sbuf,
-    cown, ctxs, cx, wog, op, otr, ofin, send_sem, recv_sem, local_sem,
+    big, transit, gbuf, xs, ssq, sqs, rsc, wg, pbuf, tr, fin, kvg, qbuf, sbuf,
+    cbig, ctransit, ctxs, wog, op, otr, ofin, send_sem, recv_sem, local_sem,
 ):
     z, y, x, c = (lax.axis_index(n) for n in ("z", "y", "x", "c"))
     zr, zl, zf = (lax.rem(z + k, 4) for k in (1, 3, 2))
@@ -71,36 +71,18 @@
     for where in partners:
         pl.semaphore_signal(barrier, inc=1, device_id=where, device_id_type=MESH)
 
-    @pl.when(x != z)
-    def _():
-        pl.semaphore_signal(barrier, inc=1, device_id={"z": x, "x": z}, device_id_type=MESH)
-
-    pl.semaphore_wait(barrier, len(partners) + jnp.where(x != z, 1, 0))
-
-    def swap_start(src, dst, name):
-        copy = message(src, dst, name, z=x, x=z)
-        local = pltpu.make_async_copy(src, dst, local_sem.at[ids(*name)])
-
-        @pl.when(x != z)
-        def _():
-            copy.start()
-
-        @pl.when(x == z)
-        def _():
-            local.start()
-
-    def swap_arrived(src, dst, name):
-        copy = message(src, dst, name, z=x, x=z)
-        local = pltpu.make_async_copy(src, dst, local_sem.at[ids(*name)])
-
-        @pl.when(x != z)
-        def _():
-            copy.wait_recv()
-            copy.wait_send()
-
-        @pl.when(x == z)
-        def _():
-            local.wait()
+    def load(src, dst, name):
+        copy = pltpu.make_async_copy(src, dst, local_sem.at[ids("load", name)])
+        copy.start()
+        return copy
+
+    weights = {"k": wk, "v": wv, "q": wq}
+    order = {"k": 0, "v": 1, "q": 2}
+    loads = {"x": load(hidden, big.at[x], "x")}
+    for name in "kvq":
+        loads[name] = load(weights[name], wg.at[order[name], y], name)
+    loads["o"] = load(wout, wog.at[y], "o")
+    pl.semaphore_wait(barrier, len(partners))
 
     def gather_y(slot, name):
         send(slot(y, None), slot(y, None), (name, "r"), y=yr)
@@ -116,8 +98,6 @@
         arrived(slot(yf, 0), (name, "fr"), y=yr)
         arrived(slot(yf, 1), (name, "fl"), y=yl)
 
-    weights = {"k": wk, "v": wv, "q": wq}
-    order = {"k": 0, "v": 1, "q": 2}
     wrows = wk.shape[0]
 
     def weight_slot(name):
@@ -126,37 +106,96 @@
             return ref if part is None else ref.at[pl.ds(part * (wrows // 2), wrows // 2)]
         return slot
 
-    def weight_gather(name):
-        mine = weights[name]
-        dst = weight_slot(name)(y, None)
-        send(mine, dst, ("w" + name, "r"), y=yr)
-        send(mine, dst, ("w" + name, "l"), y=yl)
-
-    def rows(ref, h):
-        return ref.at[pl.ds(h * half, half)]
-
-    def x_slot(plane, t, h):
-        return rows(xg.at[plane, t], h)
-
-    weight_gather("k")
-    for h in range(2):
-        swap_start(rows(hidden, h), x_slot(c, z, h), ("xp", h))
-    swap_start(gain, gbuf.at[c], ("gp",))
-    weight_gather("v")
-    local_w = []
-    for name in "kvq":
-        copy = pltpu.make_async_copy(weights[name], wg.at[order[name], y], local_sem.at[ids("lw", name)])
-        copy.start()
-        local_w.append(copy)
-
-    def process(plane, t, first):
-        g = gbuf[plane].astype(F32)
+    class Spread:
+        def __init__(self, name, buf, through):
+            self.name, self.buf, self.through = name, buf, through
+            self.rows = buf.shape[1] // 2
+
+        def part(self, slot, h):
+            return self.buf.at[slot, pl.ds(h * self.rows, self.rows)]
+
+        def own(self, h):
+            mine = self.part(x, h)
+            send(mine, mine, (self.name, "xr", h), x=xr)
+            send(mine, mine, (self.name, "xl", h), x=xl)
+            self.onward(0, h)
+
+        def pair(self, src_slot, owner, label, h):
+            send(self.part(src_slot, h), self.part(8 + owner, h), (self.name, "pair", label, h), c=other)
+
+        def onward(self, k, h):
+            owner = lax.rem(x + k, 4)
+            away = lax.rem(owner - z + 4, 4)
+            src = self.part(owner, h)
+
+            @pl.when(away == 0)
+            def _():
+                message(src, self.part(8 + z, h), (self.name, "pair", "own", h), c=other).start()
+
+            @pl.when(away == 1)
+            def _():
+                message(src, self.part(4 + z, h), (self.name, "zr", h), z=zr).start()
+
+            @pl.when(away == 3)
+            def _():
+                message(src, self.part(4 + z, h), (self.name, "zl", h), z=zl).start()
+
+            @pl.when(away == 2)
+            def _():
+                to = {"z": zl} if h else {"z": zr}
+                message(src, self.through.at[h], (self.name, "zz", h), **to).start()
+
+            if k == 0:
+                for label, where in (("zr", {"z": zr}), ("zl", {"z": zl}), ("zz", {"z": zl} if h else {"z": zr})):
+                    sends.append(message(self.part(0, h), self.part(0, h), (self.name, label, h), **where))
+                sends.append(message(self.part(0, h), self.part(0, h), (self.name, "pair", "own", h), c=other))
+
+        def from_left(self, h):
+            mine = self.part(xl, h)
+            arrived(mine, (self.name, "xr", h), x=xr)
+            if h == 0:
+                send(mine, mine, (self.name, "xf", 0), x=xr)
+            self.onward(3, h)
+
+        def from_right(self, h):
+            mine = self.part(xr, h)
+            arrived(mine, (self.name, "xl", h), x=xl)
+            if h == 1:
+                send(mine, mine, (self.name, "xf", 1), x=xl)
+            self.onward(1, h)
+
+        def from_far(self, h):
+            where = {"x": xl} if h else {"x": xr}
+            arrived(self.part(xf, h), (self.name, "xf", h), **where)
+            self.onward(2, h)
+
+        def pass_on(self, h):
+            where = {"z": zl} if h else {"z": zr}
+            arrived(self.through.at[h], (self.name, "zz", h), **where)
+            send(self.through.at[h], self.part(4 + (zr if h else zl), h), (self.name, "zf", h), **where)
+
+        def beside(self, which, h):
+            owner, where = (zl, {"z": zr}) if which == "zr" else (zr, {"z": zl})
+            arrived(self.part(4 + owner, h), (self.name, which, h), **where)
+            self.pair(4 + owner, owner, which, h)
+
+        def opposite(self, h):
+            where = {"z": zl} if h else {"z": zr}
+            arrived(self.part(4 + zf, h), (self.name, "zf", h), **where)
+            self.pair(4 + zf, zf, "zf", h)
+
+        def paired(self, owner, label):
+            for h in range(2):
+                arrived(self.part(8 + owner, h), (self.name, "pair", label, h), c=other)
+
+    def process(slot, plane, t, first):
+        g = gbuf[z, plane].astype(F32)
         width = g.shape[1]
 
         @pl.loop(0, block // 32)
         def _(i):
             r = pl.ds(pl.multiple_of(i * 32, 32), 32)
-            v = xg[plane, t, r, :].astype(F32)
+            v = big[slot, r, :].astype(F32)
             xs[plane, t, r, :] = (v * g).astype(BF)
             sq = v * v
             total = sq[:, :HD]
@@ -167,45 +206,56 @@
             else:
                 ssq[t, r, :] = ssq[t, r, :] + total
 
-    def pair_send(t, label, h):
-        send(x_slot(c, t, h), x_slot(c, t, h), ("pair", label, h), c=other)
-
-    swap_arrived(gain, gbuf.at[c], ("gp",))
-    send(gbuf.at[c], gbuf.at[c], ("gpair",), c=other)
+    spread = Spread("h", big, transit)
+    loads["x"].wait()
     for h in range(2):
-        swap_arrived(rows(hidden, h), x_slot(c, x, h), ("xp", h))
-        send(x_slot(c, x, h), x_slot(c, x, h), ("xr", h), x=xr)
-        send(x_slot(c, x, h), x_slot(c, x, h), ("xl", h), x=xl)
-        pair_send(x, "own", h)
+        spread.own(h)
+    loads["k"].wait()
+    gather_y(weight_slot("k"), "wk")
+    loads["v"].wait()
+    gather_y(weight_slot("v"), "wv")
+    gain_copy = pltpu.make_async_copy(gain, gbuf.at[x, c], local_sem.at[ids("gain")])
+    gain_copy.start()
+    gain_sends = [("r", {"x": xr}), ("l", {"x": xl}), ("c", {"c": other})]
+    for label, where in gain_sends:
+        send(gain, gbuf.at[x, c], ("gain", label), **where)
+    spread.from_left(0)
+    spread.from_right(0)
+    spread.from_right(1)
+    spread.from_left(1)
+    arrived(gbuf.at[xl, c], ("gain", "r"), x=xr)
+    send(gbuf.at[xl, c], gbuf.at[xl, c], ("gain", "rf"), x=xr)
+    send(gbuf.at[xl, c], gbuf.at[xl, c], ("gain", "rc"), c=other)
+    arrived(gbuf.at[xr, c], ("gain", "l"), x=xl)
+    send(gbuf.at[xr, c], gbuf.at[xr, c], ("gain", "lc"), c=other)
     forward_y(weight_slot("k"), "wk")
-    process(c, x, True)
-    arrived(x_slot(c, xl, 0), ("xr", 0), x=xr)
-    send(x_slot(c, xl, 0), x_slot(c, xl, 0), ("xfr",), x=xr)
-    pair_send(xl, "left", 0)
-    arrived(x_slot(c, xr, 0), ("xl", 0), x=xl)
-    pair_send(xr, "right", 0)
+    spread.from_far(0)
+    spread.from_far(1)
+    arrived(gbuf.at[xf, c], ("gain", "rf"), x=xr)
+    send(gbuf.at[xf, c], gbuf.at[xf, c], ("gain", "fc"), c=other)
+    spread.pass_on(0)
+    spread.pass_on(1)
+    gain_copy.wait()
+    arrived(gbuf.at[x, other], ("gain", "c"), c=other)
+    arrived(gbuf.at[xl, other], ("gain", "rc"), c=other)
+    arrived(gbuf.at[xr, other], ("gain", "lc"), c=other)
+    arrived(gbuf.at[xf, other], ("gain", "fc"), c=other)
+    process(z, c, z, True)
     forward_y(weight_slot("v"), "wv")
-    weight_gather("q")
-    arrived(x_slot(c, xr, 1), ("xl", 1), x=xl)
-    send(x_slot(c, xr, 1), x_slot(c, xr, 1), ("xfl",), x=xl)
-    pair_send(xr, "right", 1)
-    arrived(x_slot(c, xl, 1), ("xr", 1), x=xr)
-    pair_send(xl, "left", 1)
-    arrived(gbuf.at[other], ("gpair",), c=other)
-    process(c, xr, True)
-    process(c, xl, True)
+    loads["q"].wait()
+    gather_y(weight_slot("q"), "wq")
+    for which, owner in (("zr", zl), ("zl", zr)):
+        for h in range(2):
+            spread.beside(which, h)
+        process(4 + owner, c, owner, True)
+    spread.paired(z, "own")
+    process(8 + z, other, z, False)
     for h in range(2):
-        arrived(x_slot(other, x, h), ("pair", "own", h), c=other)
-    process(other, x, False)
-    arrived(x_slot(c, xf, 0), ("xfr",), x=xr)
-    pair_send(xf, "far", 0)
-    arrived(x_slot(c, xf, 1), ("xfl",), x=xl)
-    pair_send(xf, "far", 1)
-    process(c, xf, True)
-    for t, label in ((xr, "right"), (xl, "left"), (xf, "far")):
-        for h in range(2):
-            arrived(x_slot(other, t, h), ("pair", label, h), c=other)
-        process(other, t, False)
+        spread.opposite(h)
+    process(4 + zf, c, zf, True)
+    for label, owner in (("zr", zl), ("zl", zr), ("zf", zf)):
+        spread.paired(owner, label)
+        process(8 + owner, other, owner, False)
     for t in range(4):
         s = jnp.sum(ssq[t].T, axis=0, keepdims=True)
         sqs[z, t] = jnp.broadcast_to(s, (8, block))
@@ -237,6 +287,8 @@
             pbuf[j, 2 * n] = acc[:, :HD].astype(BF)
             pbuf[j, 2 * n + 1] = acc[:, HD:].astype(BF)
 
+    def scatter(name):
+        j = order[name]
         send(lower(pbuf.at[j, zf]), tr.at[j, 0], (name, "ta"), z=zr)
         send(upper(pbuf.at[j, zf]), tr.at[j, 1], (name, "tb"), z=zl)
         send(upper(pbuf.at[j, zr]), upper(fin.at[j, 0]), (name, "a1"), z=zr)
@@ -277,14 +329,13 @@
         signed = jnp.where(lane < HD // 2, -sin, sin)
         return v * cos + pltpu.roll(v, HD // 2, axis=1) * signed
 
-    for copy in local_w:
-        copy.wait()
     finish_y(weight_slot("k"), "wk")
     project("k")
+    scatter("k")
     finish_y(weight_slot("v"), "wv")
     project("v")
-    forward_y(weight_slot("q"), "wq")
     relay("k")
+    scatter("v")
 
     for where, label in ((zr, 1), (zl, 3), (zf, 2)):
         src = {1: zl, 3: zr, 2: zf}[label]
@@ -305,13 +356,15 @@
         count = wout.shape[0] // 2
         return ref if part is None else ref.at[pl.ds(part * count, count)]
 
-    relay("v")
+    forward_y(weight_slot("q"), "wq")
     reduced("k")
     for t in range(4):
         kvg[0, t, y] = rotated(total_of("k", t), t).astype(BF)
     gather_y(kv_slot(0), "k")
+    relay("v")
     finish_y(weight_slot("q"), "wq")
     project("q")
+    scatter("q")
     reduced("v")
     for t in range(4):
         kvg[1, t, y] = total_of("v", t).astype(BF)
@@ -319,10 +372,8 @@
     relay("q")
     forward_y(kv_slot(0), "k")
     forward_y(kv_slot(1), "v")
-    send(wout, wog.at[y], ("wo", "r"), y=yr)
-    send(wout, wog.at[y], ("wo", "l"), y=yl)
-    wo_copy = pltpu.make_async_copy(wout, wog.at[y], local_sem.at[ids("lwo")])
-    wo_copy.start()
+    loads["o"].wait()
+    gather_y(out_slot, "wo")
     reduced("q")
     for t in range(4):
         qbuf[t] = rotated(total_of("q", t), t).astype(BF)
@@ -335,9 +386,6 @@
     def keys(which, kb):
         return kvg[which, kb].reshape(span, HD)
 
-    def cx_slot(plane, owner, t):
-        return cx.at[plane, owner, pl.ds(t * block, block)]
-
     heads_base = [ids("c2", k) for k in range(4)][0]
 
     def head_copy(src, dst, target, source):
@@ -347,7 +395,7 @@
         )
 
     def context_sends(t):
-        mine = cown.at[pl.ds(t * block, block)]
+        mine = cbig.at[x, pl.ds(t * block, block)]
 
         @pl.when(z != t)
         def _():
@@ -355,10 +403,9 @@
 
         @pl.when(z == t)
         def _():
-            ctxs[z] = cown[pl.ds(t * block, block), :]
-
-        swap_start(mine, cx_slot(c, z, t), ("cp", t))
-
+            ctxs[z] = cbig[x, pl.ds(t * block, block), :]
+
+    around = Spread("c", cbig, ctransit)
     for t in range(4):
         q = qbuf[t]
 
@@ -387,59 +434,47 @@
         total, acc = lax.fori_loop(
             0, t + 1, weigh, (jnp.zeros((block, 1), F32), jnp.zeros((block, HD), F32))
         )
-        cown[pl.ds(t * block, block), :] = (acc / total).astype(BF)
+        cbig[x, pl.ds(t * block, block), :] = (acc / total).astype(BF)
+        if t % 2 == 1:
+            around.own(t // 2)
         context_sends(t)
-        if t == 1:
-            forward_y(out_slot, "wo")
-
-    def cx_part(plane, owner, h):
-        return cx.at[plane, owner, pl.ds(2 * h * block, 2 * block)]
-
+        if t == 2:
+            around.from_left(0)
+            around.from_right(0)
+
+    around.from_right(1)
+    around.from_left(1)
+    around.from_far(0)
+    around.from_far(1)
+    around.pass_on(0)
+    around.pass_on(1)
+    forward_y(out_slot, "wo")
+    for which in ("zr", "zl"):
+        for h in range(2):
+            around.beside(which, h)
     for h in range(2):
-        for t in (2 * h, 2 * h + 1):
-            mine = cown.at[pl.ds(t * block, block)]
-            swap_arrived(mine, cx_slot(c, x, t), ("cp", t))
-        send(cx_part(c, x, h), cx_part(c, x, h), ("cr", h), x=xr)
-        send(cx_part(c, x, h), cx_part(c, x, h), ("cl", h), x=xl)
-        send(cx_part(c, x, h), cx_part(c, x, h), ("cpair", "own", h), c=other)
-
-    def cx_pair(owner, label, h):
-        send(cx_part(c, owner, h), cx_part(c, owner, h), ("cpair", label, h), c=other)
-
-    arrived(cx_part(c, xl, 0), ("cr", 0), x=xr)
-    send(cx_part(c, xl, 0), cx_part(c, xl, 0), ("cfr",), x=xr)
-    cx_pair(xl, "left", 0)
-    arrived(cx_part(c, xr, 0), ("cl", 0), x=xl)
-    cx_pair(xr, "right", 0)
-    arrived(cx_part(c, xr, 1), ("cl", 1), x=xl)
-    send(cx_part(c, xr, 1), cx_part(c, xr, 1), ("cfl",), x=xl)
-    cx_pair(xr, "right", 1)
-    arrived(cx_part(c, xl, 1), ("cr", 1), x=xr)
-    cx_pair(xl, "left", 1)
+        around.opposite(h)
 
     for h in range(4):
         @pl.when(z != h)
         def _():
-            copy = head_copy(cown.at[pl.ds(h * block, block)], ctxs.at[h], h, h)
+            copy = head_copy(ctxs.at[h], ctxs.at[h], h, h)
             copy.wait_send()
             copy.wait_recv()
 
     for h in range(4):
         ctx_out[:, h * HD:(h + 1) * HD] = ctxs[h]
 
-    wo_copy.wait()
     finish_y(out_slot, "wo")
-    arrived(cx_part(c, xf, 0), ("cfr",), x=xr)
-    cx_pair(xf, "far", 0)
-    arrived(cx_part(c, xf, 1), ("cfl",), x=xl)
-    cx_pair(xf, "far", 1)
-    for label, owner in (("own", x), ("left", xl), ("right", xr), ("far", xf)):
-        for h in range(2):
-            arrived(cx_part(other, owner, h), ("cpair", label, h), c=other)
+    for label, owner in (("own", z), ("zr", zl), ("zl", zr), ("zf", zf)):
+        around.paired(owner, label)
 
     def out_product(d):
         r = pl.ds(pl.multiple_of(d * block, block), block)
-        left = jnp.concatenate([cx[p, k, r, :] for p in range(2) for k in range(4)], axis=1)
+        slots = [
+            jnp.where(c == p, jnp.where(z == k, k, 4 + k), 8 + k) for p in range(2) for k in range(4)
+        ]
+        left = jnp.concatenate([cbig[slot, r, :] for slot in slots], axis=1)
         right = wog[...].reshape(left.shape[1], wog.shape[2])
         return jnp.dot(left, right, preferred_element_type=F32)
 
@@ -463,7 +498,7 @@
     arrived(otr.at[1], ("o", "tb"), z=zl)
     op[zl, hi, :] = (op[zl, hi, :].astype(F32) + otr[1].astype(F32)).astype(BF)
     send(second(op.at[zl]), second(ofin.at[1]), ("o", "b1"), z=zl)
-    oacc = hidden[...].astype(F32) + out_product(z)
+    oacc = big[x].astype(F32) + out_product(z)
     arrived(second(ofin.at[0]), ("o", "a1"), z=zr)
     arrived(first(ofin.at[1]), ("o", "b0"), z=zl)
     arrived(first(ofin.at[0]), ("o", "a0"), z=zr)
@@ -490,11 +525,12 @@
             jax.ShapeDtypeStruct((block, cw), BF),
             jax.ShapeDtypeStruct((block, ow), BF),
         ),
-        in_specs=[vmem] * 7,
+        in_specs=[pl.BlockSpec(memory_space=pl.ANY)] * 5 + [vmem] * 2,
         out_specs=(vmem, vmem),
         scratch_shapes=[
-            pltpu.VMEM((2, 4, block, width), BF),
-            pltpu.VMEM((2, 1, width), BF),
+            pltpu.VMEM((12, block, width), BF),
+            pltpu.VMEM((2, block // 2, width), BF),
+            pltpu.VMEM((4, 2, 1, width), BF),
             pltpu.VMEM((2, 4, block, width), BF),
             pltpu.VMEM((4, block, HD), F32),
             pltpu.VMEM((4, 4, 8, block), F32),
@@ -506,9 +542,9 @@
             pltpu.VMEM((2, 4, 4, block, HD), BF),
             pltpu.VMEM((4, block, HD), BF),
             pltpu.VMEM((4, block, 4 * block), F32),
-            pltpu.VMEM((4 * block, HD), BF),
+            pltpu.VMEM((12, 4 * block, HD), BF),
+            pltpu.VMEM((2, 2 * block, HD), BF),
             pltpu.VMEM((4, block, HD), BF),
-            pltpu.VMEM((2, 4, 4 * block, HD), BF),
             pltpu.VMEM((4, orows, ow), BF),
             pltpu.VMEM((4, block, ow), BF),
             pltpu.VMEM((2, block // 2, ow), BF),
@@ -520,7 +556,7 @@
         compiler_params=pltpu.CompilerParams(
             collective_id=0, has_side_effects=True, vmem_limit_bytes=62 * 1024 * 1024
         ),
-    )(hidden, norm_gain.reshape(1, width), w_query, w_key, w_value, w_out, tables)
+    )(hidden, w_query, w_key, w_value, w_out, norm_gain.reshape(1, width), tables)
 
 
 def solution(mesh):

time: 156 us -> 140 us (0.90)
  Pallas kernels: 150 us -> 135 us
    pallas_call x1, Pallas kernels: 150 us -> 135 us  [on_device(): pl.pallas_call(body, out_shape=(jax.ShapeDtypeStruct((block, cw), BF), ja...]
where the time goes in v2:
time: 140 us; the launch traced here: 139 us
  Pallas kernels  135 us (96%)
  local copies, waits for them, and re-layouts  3.8 us (3%)
    pallas_call x1, Pallas kernels, on_device(): pl.pallas_call(body, out_shape=(jax.ShapeDtypeStruct((block, cw), BF), ja...  135 us

profile of v2, /device:TPU:1, one launch (start us, length us, event | category | flops | bytes accessed | tf_op | source)
XLA Modules:
  0.0 139.0 jit_solution(3739247120552820381)
XLA Ops:
  0.6 1.3 reshape.7.refs_5_
  1.9 134.5 %shard_map.86 = (bf16[256,512]{1,0:T(8,128)(2,1)}, bf16[256,1024]{1,0:T(8,128)(2,1)}) custom-call(bf16[256,1024]{1,0:T(8,128)(2,1)} %refs_0_.1, bf16[512,512]{1,0:T(8,128)(2,1)} %refs_1_.1, bf16[512,512]{1,0:T(8,128)(2,1)} %refs_2_.1, bf16[512,512]{1,0:T(8,128)(2,1)} %refs_3_.1, bf16[256,1024]{1,0:T(8,128)(2,1)} %refs_4_.1, bf16[1,1024]{1,0:T(2,128)(2,1)} %reshape.7.refs_5_, ...), custom_call_target="tpu_custom_call" | custom-call | tf_op jit(solution)/shard_map/pallas_call | solution.py:522
  136.4 0.0 copy-start
  136.5 1.7 %copy.11 = bf16[256,512]{1,0:T(8,128)(2,1)} copy(bf16[256,512]{1,0:T(8,128)(2,1)} %get-tuple-element.4) | data formatting | bytes 524288
  138.2 0.0 copy-done
  138.2 0.8 copy.12
Async XLA Ops:
  136.4 1.7 %copy-start = (bf16[256,1024]{1,0:T(8,128)(2,1)S(1)}, bf16[256,1024]{1,0:T(8,128)(2,1)}, u32[]{:S(2)}) copy-start(bf16[256,1024]{1,0:T(8,128)(2,1)} %get-tuple-element.5) | copy-start | bytes 1572868

commit v3 on v2

--- a/solution.py
+++ b/solution.py
@@ -39,7 +39,7 @@
     features, hidden, wq, wk, wv, wout, gain, tables,
     ctx_out, layer_out,
     big, transit, gbuf, xs, ssq, sqs, rsc, wg, pbuf, tr, fin, kvg, qbuf, sbuf,
-    cbig, ctransit, ctxs, wog, op, otr, ofin, send_sem, recv_sem, local_sem,
+    probs, cown, cx, ctxs, wog, op, otr, ofin, oacc, lout, send_sem, recv_sem, local_sem,
 ):
     z, y, x, c = (lax.axis_index(n) for n in ("z", "y", "x", "c"))
     zr, zl, zf = (lax.rem(z + k, 4) for k in (1, 3, 2))
@@ -81,22 +81,36 @@
     loads = {"x": load(hidden, big.at[x], "x")}
     for name in "kvq":
         loads[name] = load(weights[name], wg.at[order[name], y], name)
-    loads["o"] = load(wout, wog.at[y], "o")
+    loads["o"] = load(wout, wog.at[z], "o")
     pl.semaphore_wait(barrier, len(partners))
 
+    lines = {"y": (y, yr, yl, yf), "z": (z, zr, zl, zf)}
+
+    def gather(axis, slot, name):
+        me, right, left, _ = lines[axis]
+        send(slot(me, None), slot(me, None), (name, "r"), **{axis: right})
+        send(slot(me, None), slot(me, None), (name, "l"), **{axis: left})
+
+    def forward(axis, slot, name):
+        _, right, left, _ = lines[axis]
+        arrived(slot(left, None), (name, "r"), **{axis: right})
+        send(slot(left, 0), slot(left, 0), (name, "fr"), **{axis: right})
+        arrived(slot(right, None), (name, "l"), **{axis: left})
+        send(slot(right, 1), slot(right, 1), (name, "fl"), **{axis: left})
+
+    def finish(axis, slot, name):
+        _, right, left, far = lines[axis]
+        arrived(slot(far, 0), (name, "fr"), **{axis: right})
+        arrived(slot(far, 1), (name, "fl"), **{axis: left})
+
     def gather_y(slot, name):
-        send(slot(y, None), slot(y, None), (name, "r"), y=yr)
-        send(slot(y, None), slot(y, None), (name, "l"), y=yl)
+        gather("y", slot, name)
 
     def forward_y(slot, name):
-        arrived(slot(yl, None), (name, "r"), y=yr)
-        send(slot(yl, 0), slot(yl, 0), (name, "fr"), y=yr)
-        arrived(slot(yr, None), (name, "l"), y=yl)
-        send(slot(yr, 1), slot(yr, 1), (name, "fl"), y=yl)
+        forward("y", slot, name)
 
     def finish_y(slot, name):
-        arrived(slot(yf, 0), (name, "fr"), y=yr)
-        arrived(slot(yf, 1), (name, "fl"), y=yl)
+        finish("y", slot, name)
 
     wrows = wk.shape[0]
 
@@ -370,15 +384,14 @@
         kvg[1, t, y] = total_of("v", t).astype(BF)
     gather_y(kv_slot(1), "v")
     relay("q")
+    loads["o"].wait()
+    gather("z", out_slot, "wo")
     forward_y(kv_slot(0), "k")
     forward_y(kv_slot(1), "v")
-    loads["o"].wait()
-    gather_y(out_slot, "wo")
     reduced("q")
     for t in range(4):
         qbuf[t] = rotated(total_of("q", t), t).astype(BF)
     finish_y(kv_slot(0), "k")
-    finish_y(kv_slot(1), "v")
 
     factor = math.log2(math.e) / math.sqrt(HD)
     span = 4 * block
@@ -386,26 +399,17 @@
     def keys(which, kb):
         return kvg[which, kb].reshape(span, HD)
 
-    heads_base = [ids("c2", k) for k in range(4)][0]
-
-    def head_copy(src, dst, target, source):
+    def base_of(name):
+        return [ids(name, k) for k in range(4)][0]
+
+    def direct(src, dst, name, to, source, **where):
+        first = base_of(name)
         return pltpu.make_async_remote_copy(
-            src_ref=src, dst_ref=dst, send_sem=send_sem.at[heads_base + target],
-            recv_sem=recv_sem.at[heads_base + source], device_id={"z": target}, device_id_type=MESH,
+            src_ref=src, dst_ref=dst, send_sem=send_sem.at[first + to],
+            recv_sem=recv_sem.at[first + source], device_id=where, device_id_type=MESH,
         )
 
-    def context_sends(t):
-        mine = cbig.at[x, pl.ds(t * block, block)]
-
-        @pl.when(z != t)
-        def _():
-            head_copy(mine, ctxs.at[z], t, z).start()
-
-        @pl.when(z == t)
-        def _():
-            ctxs[z] = cbig[x, pl.ds(t * block, block), :]
-
-    around = Spread("c", cbig, ctransit)
+    sums = []
     for t in range(4):
         q = qbuf[t]
 
@@ -423,58 +427,108 @@
         s = jnp.where(col <= row, s, -jnp.inf)
         sbuf[t] = s
         peak = jnp.maximum(peak, jnp.max(s, axis=1, keepdims=True))
-
-        def weigh(kb, carry):
-            total, acc = carry
+        place = t * (t + 1) // 2
+
+        def weigh(kb, total):
             p = jnp.exp2((sbuf[kb] - peak) * factor)
-            total = total + jnp.sum(p, axis=1, keepdims=True)
-            acc = acc + jnp.dot(p.astype(BF), keys(1, kb), preferred_element_type=F32)
-            return total, acc
-
-        total, acc = lax.fori_loop(
-            0, t + 1, weigh, (jnp.zeros((block, 1), F32), jnp.zeros((block, HD), F32))
-        )
-        cbig[x, pl.ds(t * block, block), :] = (acc / total).astype(BF)
-        if t % 2 == 1:
-            around.own(t // 2)
-        context_sends(t)
-        if t == 2:
-            around.from_left(0)
-            around.from_right(0)
-
-    around.from_right(1)
-    around.from_left(1)
-    around.from_far(0)
-    around.from_far(1)
-    around.pass_on(0)
-    around.pass_on(1)
-    forward_y(out_slot, "wo")
-    for which in ("zr", "zl"):
-        for h in range(2):
-            around.beside(which, h)
+            probs[place + kb] = p.astype(BF)
+            return total + jnp.sum(p, axis=1, keepdims=True)
+
+        sums.append(lax.fori_loop(0, t + 1, weigh, jnp.zeros((block, 1), F32)))
+
+    to_y, to_c = 2 * c + z // 2, lax.rem(z, 2)
+    from_z, from_c = 2 * lax.rem(y, 2), y // 2
+    finish_y(kv_slot(1), "v")
+    for t in range(4):
+        place = t * (t + 1) // 2
+
+        def add(kb, acc):
+            return acc + jnp.dot(probs[place + kb], keys(1, kb), preferred_element_type=F32)
+
+        acc = lax.fori_loop(0, t + 1, add, jnp.zeros((block, HD), F32))
+        cown[t] = (acc / sums[t]).astype(BF)
+        itself = jnp.logical_and(z == t, jnp.logical_and(to_y == y, to_c == c))
+
+        @pl.when(jnp.logical_not(itself))
+        def _():
+            direct(cown.at[t], cx.at[to_c, x, y], "cd", t, y, z=t, y=to_y, c=to_c).start()
+
+        @pl.when(itself)
+        def _():
+            cx[c, x, y] = cown[t]
+
+    for t in range(4):
+        @pl.when(z != t)
+        def _():
+            direct(cown.at[t], ctxs.at[z], "c2", t, z, z=t).start()
+
+        @pl.when(z == t)
+        def _():
+            ctxs[z] = cown[t]
+
+    forward("z", out_slot, "wo")
+
+    def cx_part(plane, owner, h):
+        return cx.at[plane, owner, pl.ds(2 * h, 2)]
+
+    def cx_pair(owner, label, h):
+        send(cx_part(c, owner, h), cx_part(c, owner, h), ("cp", label, h), c=other)
+
     for h in range(2):
-        around.opposite(h)
-
+        for source in (2 * h, 2 * h + 1):
+            source_z = from_z + c
+            itself = jnp.logical_and(source == y, jnp.logical_and(source_z == z, from_c == c))
+
+            @pl.when(jnp.logical_not(itself))
+            def _():
+                direct(cx.at[c, x, source], cx.at[c, x, source], "cd", source, source, z=z).wait_recv()
+
+        send(cx_part(c, x, h), cx_part(c, x, h), ("cr", h), x=xr)
+        send(cx_part(c, x, h), cx_part(c, x, h), ("cl", h), x=xl)
+        cx_pair(x, "own", h)
+    for t in range(4):
+        itself = jnp.logical_and(z == t, jnp.logical_and(to_y == y, to_c == c))
+
+        @pl.when(jnp.logical_not(itself))
+        def _():
+            direct(cown.at[t], cown.at[t], "cd", t, t, z=z).wait_send()
+
+    arrived(cx_part(c, xl, 0), ("cr", 0), x=xr)
+    send(cx_part(c, xl, 0), cx_part(c, xl, 0), ("cf", 0), x=xr)
+    cx_pair(xl, "left", 0)
+    arrived(cx_part(c, xr, 0), ("cl", 0), x=xl)
+    cx_pair(xr, "right", 0)
+    arrived(cx_part(c, xr, 1), ("cl", 1), x=xl)
+    send(cx_part(c, xr, 1), cx_part(c, xr, 1), ("cf", 1), x=xl)
+    cx_pair(xr, "right", 1)
+    arrived(cx_part(c, xl, 1), ("cr", 1), x=xr)
+    cx_pair(xl, "left", 1)
+
+    context_out = []
     for h in range(4):
         @pl.when(z != h)
         def _():
-            copy = head_copy(ctxs.at[h], ctxs.at[h], h, h)
+            copy = direct(ctxs.at[h], ctxs.at[h], "c2", h, h, z=h)
             copy.wait_send()
             copy.wait_recv()
 
-    for h in range(4):
-        ctx_out[:, h * HD:(h + 1) * HD] = ctxs[h]
-
-    finish_y(out_slot, "wo")
-    for label, owner in (("own", z), ("zr", zl), ("zl", zr), ("zf", zf)):
-        around.paired(owner, label)
+        copy = pltpu.make_async_copy(
+            ctxs.at[h], ctx_out.at[:, pl.ds(h * HD, HD)], local_sem.at[ids("ctx", h)]
+        )
+        copy.start()
+        context_out.append(copy)
+
+    finish("z", out_slot, "wo")
+    arrived(cx_part(c, xf, 0), ("cf", 0), x=xr)
+    cx_pair(xf, "far", 0)
+    arrived(cx_part(c, xf, 1), ("cf", 1), x=xl)
+    cx_pair(xf, "far", 1)
+    for label, owner in (("own", x), ("left", xl), ("right", xr), ("far", xf)):
+        for h in range(2):
+            arrived(cx_part(other, owner, h), ("cp", label, h), c=other)
 
     def out_product(d):
-        r = pl.ds(pl.multiple_of(d * block, block), block)
-        slots = [
-            jnp.where(c == p, jnp.where(z == k, k, 4 + k), 8 + k) for p in range(2) for k in range(4)
-        ]
-        left = jnp.concatenate([cbig[slot, r, :] for slot in slots], axis=1)
+        left = jnp.concatenate([cx[p, k, d] for k in range(4) for p in range(2)], axis=1)
         right = wog[...].reshape(left.shape[1], wog.shape[2])
         return jnp.dot(left, right, preferred_element_type=F32)
 
@@ -484,28 +538,35 @@
     def second(ref):
         return ref.at[pl.ds(half, half)]
 
-    op[zf] = out_product(zf).astype(BF)
-    send(first(op.at[zf]), otr.at[0], ("o", "ta"), z=zr)
-    send(second(op.at[zf]), otr.at[1], ("o", "tb"), z=zl)
-    op[zr] = out_product(zr).astype(BF)
-    send(second(op.at[zr]), second(ofin.at[0]), ("o", "a1"), z=zr)
-    op[zl] = out_product(zl).astype(BF)
-    send(first(op.at[zl]), first(ofin.at[1]), ("o", "b0"), z=zl)
+    op[yf] = out_product(yf).astype(BF)
+    send(first(op.at[yf]), otr.at[0], ("o", "ta"), y=yr)
+    send(second(op.at[yf]), otr.at[1], ("o", "tb"), y=yl)
+    op[yr] = out_product(yr).astype(BF)
+    send(second(op.at[yr]), second(ofin.at[0]), ("o", "a1"), y=yr)
+    op[yl] = out_product(yl).astype(BF)
+    send(first(op.at[yl]), first(ofin.at[1]), ("o", "b0"), y=yl)
     lo, hi = pl.ds(0, half), pl.ds(half, half)
-    arrived(otr.at[0], ("o", "ta"), z=zr)
-    op[zr, lo, :] = (op[zr, lo, :].astype(F32) + otr[0].astype(F32)).astype(BF)
-    send(first(op.at[zr]), first(ofin.at[0]), ("o", "a0"), z=zr)
-    arrived(otr.at[1], ("o", "tb"), z=zl)
-    op[zl, hi, :] = (op[zl, hi, :].astype(F32) + otr[1].astype(F32)).astype(BF)
-    send(second(op.at[zl]), second(ofin.at[1]), ("o", "b1"), z=zl)
-    oacc = big[x].astype(F32) + out_product(z)
-    arrived(second(ofin.at[0]), ("o", "a1"), z=zr)
-    arrived(first(ofin.at[1]), ("o", "b0"), z=zl)
-    arrived(first(ofin.at[0]), ("o", "a0"), z=zr)
-    arrived(second(ofin.at[1]), ("o", "b1"), z=zl)
-    layer_out[...] = (oacc + ofin[0].astype(F32) + ofin[1].astype(F32)).astype(BF)
+    arrived(otr.at[0], ("o", "ta"), y=yr)
+    op[yr, lo, :] = (op[yr, lo, :].astype(F32) + otr[0].astype(F32)).astype(BF)
+    send(first(op.at[yr]), first(ofin.at[0]), ("o", "a0"), y=yr)
+    arrived(otr.at[1], ("o", "tb"), y=yl)
+    op[yl, hi, :] = (op[yl, hi, :].astype(F32) + otr[1].astype(F32)).astype(BF)
+    send(second(op.at[yl]), second(ofin.at[1]), ("o", "b1"), y=yl)
+    oacc[...] = big[x].astype(F32) + out_product(y)
+    arrived(second(ofin.at[0]), ("o", "a1"), y=yr)
+    arrived(first(ofin.at[1]), ("o", "b0"), y=yl)
+    out_copies = []
+    for h, side, name, where in ((0, 0, "a0", {"y": yr}), (1, 1, "b1", {"y": yl})):
+        r = pl.ds(h * half, half)
+        arrived(ofin.at[side, r], ("o", name), **where)
+        lout[r, :] = (oacc[r, :] + ofin[0, r, :].astype(F32) + ofin[1, r, :].astype(F32)).astype(BF)
+        copy = pltpu.make_async_copy(lout.at[r], layer_out.at[r], local_sem.at[ids("lout", h)])
+        copy.start()
+        out_copies.append(copy)
     for copy in sends:
         copy.wait_send()
+    for copy in context_out + out_copies:
+        copy.wait()
 
 
 def on_device(hidden, norm_gain, w_query, w_key, w_value, w_out):
@@ -526,7 +587,7 @@
             jax.ShapeDtypeStruct((block, ow), BF),
         ),
         in_specs=[pl.BlockSpec(memory_space=pl.ANY)] * 5 + [vmem] * 2,
-        out_specs=(vmem, vmem),
+        out_specs=(pl.BlockSpec(memory_space=pl.ANY),) * 2,
         scratch_shapes=[
             pltpu.VMEM((12, block, width), BF),
             pltpu.VMEM((2, block // 2, width), BF),
@@ -542,13 +603,16 @@
             pltpu.VMEM((2, 4, 4, block, HD), BF),
             pltpu.VMEM((4, block, HD), BF),
             pltpu.VMEM((4, block, 4 * block), F32),
-            pltpu.VMEM((12, 4 * block, HD), BF),
-            pltpu.VMEM((2, 2 * block, HD), BF),
+            pltpu.VMEM((10, block, 4 * block), BF),
+            pltpu.VMEM((4, block, HD), BF),
+            pltpu.VMEM((2, 4, 4, block, HD), BF),
             pltpu.VMEM((4, block, HD), BF),
             pltpu.VMEM((4, orows, ow), BF),
             pltpu.VMEM((4, block, ow), BF),
             pltpu.VMEM((2, block // 2, ow), BF),
             pltpu.VMEM((2, block, ow), BF),
+            pltpu.VMEM((block, ow), F32),
+            pltpu.VMEM((block, ow), BF),
             pltpu.SemaphoreType.DMA((N_MESSAGES,)),
             pltpu.SemaphoreType.DMA((N_MESSAGES,)),
             pltpu.SemaphoreType.DMA((N_MESSAGES,)),

time: 140 us -> 137 us (0.979)
  Pallas kernels: 135 us -> 132 us
    pallas_call x1, Pallas kernels: 135 us -> 132 us  [on_device(): pl.pallas_call(body, out_shape=(jax.ShapeDtypeStruct((block, cw), BF), ja...]
where the time goes in v3:
time: 137 us
  Pallas kernels  132 us (96%)
  local copies, waits for them, and re-layouts  3.8 us (3%)
    pallas_call x1, Pallas kernels, on_device(): pl.pallas_call(body, out_shape=(jax.ShapeDtypeStruct((block, cw), BF), ja...  132 us

profile of v3, /device:TPU:1, one launch (start us, length us, event | category | flops | bytes accessed | tf_op | source)
XLA Modules:
  0.0 136.8 jit_solution(6350328949741282748)
XLA Ops:
  0.6 1.3 reshape.7.refs_5_
  1.9 132.4 %shard_map.86 = (bf16[256,512]{1,0:T(8,128)(2,1)}, bf16[256,1024]{1,0:T(8,128)(2,1)}) custom-call(bf16[256,1024]{1,0:T(8,128)(2,1)} %refs_0_.1, bf16[512,512]{1,0:T(8,128)(2,1)} %refs_1_.1, bf16[512,512]{1,0:T(8,128)(2,1)} %refs_2_.1, bf16[512,512]{1,0:T(8,128)(2,1)} %refs_3_.1, bf16[256,1024]{1,0:T(8,128)(2,1)} %refs_4_.1, bf16[1,1024]{1,0:T(2,128)(2,1)} %reshape.7.refs_5_, ...), custom_call_target="tpu_custom_call" | custom-call | tf_op jit(solution)/shard_map/pallas_call | solution.py:583
  134.3 0.0 copy-start
  134.3 1.7 %copy.11 = bf16[256,512]{1,0:T(8,128)(2,1)} copy(bf16[256,512]{1,0:T(8,128)(2,1)} %get-tuple-element.4) | data formatting | bytes 524288
  136.0 0.0 copy-done
  136.0 0.8 copy.12
Async XLA Ops:
  134.3 1.7 %copy-start = (bf16[256,1024]{1,0:T(8,128)(2,1)S(1)}, bf16[256,1024]{1,0:T(8,128)(2,1)}, u32[]{:S(2)}) copy-start(bf16[256,1024]{1,0:T(8,128)(2,1)} %get-tuple-element.5) | copy-start | bytes 1572868

commit v4 on v3

--- a/solution.py
+++ b/solution.py
@@ -32,14 +32,15 @@
         return self.table.setdefault(name, len(self.table))
 
 
-N_MESSAGES = 160
+N_MESSAGES = 138
+N_LOCAL = 14
 
 
 def kernel(
     features, hidden, wq, wk, wv, wout, gain, tables,
     ctx_out, layer_out,
     big, transit, gbuf, xs, ssq, sqs, rsc, wg, pbuf, tr, fin, kvg, qbuf, sbuf,
-    probs, cown, cx, ctxs, wog, op, otr, ofin, oacc, lout, send_sem, recv_sem, local_sem,
+    probs, cown, cx, ctxs, wog, lhs, op, otr, ofin, oacc, lout, send_sem, recv_sem, local_sem,
 ):
     z, y, x, c = (lax.axis_index(n) for n in ("z", "y", "x", "c"))
     zr, zl, zf = (lax.rem(z + k, 4) for k in (1, 3, 2))
@@ -48,7 +49,7 @@
     other = 1 - c
     block = hidden.shape[0]
     half = block // 2
-    ids = Ids()
+    ids, local_ids = Ids(), Ids()
     sends = []
 
     def message(src, dst, name, **where):
@@ -72,7 +73,7 @@
         pl.semaphore_signal(barrier, inc=1, device_id=where, device_id_type=MESH)
 
     def load(src, dst, name):
-        copy = pltpu.make_async_copy(src, dst, local_sem.at[ids("load", name)])
+        copy = pltpu.make_async_copy(src, dst, local_sem.at[local_ids("load", name)])
         copy.start()
         return copy
 
@@ -88,18 +89,20 @@
 
     def gather(axis, slot, name):
         me, right, left, _ = lines[axis]
-        send(slot(me, None), slot(me, None), (name, "r"), **{axis: right})
-        send(slot(me, None), slot(me, None), (name, "l"), **{axis: left})
+        for h, side, to in ((0, "r", right), (1, "l", left), (1, "r", right), (0, "l", left)):
+            send(slot(me, h), slot(me, h), (name, side, h), **{axis: to})
 
     def forward(axis, slot, name):
         _, right, left, _ = lines[axis]
-        arrived(slot(left, None), (name, "r"), **{axis: right})
+        arrived(slot(left, 0), (name, "r", 0), **{axis: right})
         send(slot(left, 0), slot(left, 0), (name, "fr"), **{axis: right})
-        arrived(slot(right, None), (name, "l"), **{axis: left})
+        arrived(slot(right, 1), (name, "l", 1), **{axis: left})
         send(slot(right, 1), slot(right, 1), (name, "fl"), **{axis: left})
 
     def finish(axis, slot, name):
         _, right, left, far = lines[axis]
+        arrived(slot(left, 1), (name, "r", 1), **{axis: right})
+        arrived(slot(right, 0), (name, "l", 0), **{axis: left})
         arrived(slot(far, 0), (name, "fr"), **{axis: right})
         arrived(slot(far, 1), (name, "fl"), **{axis: left})
 
@@ -228,7 +231,7 @@
     gather_y(weight_slot("k"), "wk")
     loads["v"].wait()
     gather_y(weight_slot("v"), "wv")
-    gain_copy = pltpu.make_async_copy(gain, gbuf.at[x, c], local_sem.at[ids("gain")])
+    gain_copy = pltpu.make_async_copy(gain, gbuf.at[x, c], local_sem.at[local_ids("gain")])
     gain_copy.start()
     gain_sends = [("r", {"x": xr}), ("l", {"x": xl}), ("c", {"c": other})]
     for label, where in gain_sends:
@@ -379,6 +382,7 @@
     finish_y(weight_slot("q"), "wq")
     project("q")
     scatter("q")
+    forward_y(kv_slot(0), "k")
     reduced("v")
     for t in range(4):
         kvg[1, t, y] = total_of("v", t).astype(BF)
@@ -386,7 +390,6 @@
     relay("q")
     loads["o"].wait()
     gather("z", out_slot, "wo")
-    forward_y(kv_slot(0), "k")
     forward_y(kv_slot(1), "v")
     reduced("q")
     for t in range(4):
@@ -400,7 +403,7 @@
         return kvg[which, kb].reshape(span, HD)
 
     def base_of(name):
-        return [ids(name, k) for k in range(4)][0]
+        return [ids(*name, k) for k in range(4)][0]
 
     def direct(src, dst, name, to, source, **where):
         first = base_of(name)
@@ -409,163 +412,214 @@
             recv_sem=recv_sem.at[first + source], device_id=where, device_id_type=MESH,
         )
 
-    sums = []
-    for t in range(4):
-        q = qbuf[t]
-
-        def score(kb, peak):
-            s = lax.dot_general(q, keys(0, kb), (((1,), (1,)), ((), ())), preferred_element_type=F32)
-            sbuf[kb] = s
-            return jnp.maximum(peak, jnp.max(s, axis=1, keepdims=True))
-
-        peak = jnp.full((block, 1), -1e30, F32)
-        if t > 0:
-            peak = lax.fori_loop(0, t, score, peak)
-        s = lax.dot_general(q, keys(0, t), (((1,), (1,)), ((), ())), preferred_element_type=F32)
-        row = lax.broadcasted_iota(jnp.int32, (block, span), 0) + y * block
-        col = lax.broadcasted_iota(jnp.int32, (block, span), 1)
-        s = jnp.where(col <= row, s, -jnp.inf)
-        sbuf[t] = s
-        peak = jnp.maximum(peak, jnp.max(s, axis=1, keepdims=True))
-        place = t * (t + 1) // 2
-
-        def weigh(kb, total):
-            p = jnp.exp2((sbuf[kb] - peak) * factor)
-            probs[place + kb] = p.astype(BF)
-            return total + jnp.sum(p, axis=1, keepdims=True)
-
-        sums.append(lax.fori_loop(0, t + 1, weigh, jnp.zeros((block, 1), F32)))
-
     to_y, to_c = 2 * c + z // 2, lax.rem(z, 2)
-    from_z, from_c = 2 * lax.rem(y, 2), y // 2
+    from_z, from_c = 2 * lax.rem(y, 2) + c, y // 2
+
+    def rows_of(part):
+        return pl.ds(part * half, half)
+
+    def score_rows(part):
+        mine = rows_of(part)
+        sums = []
+        for t in range(4):
+            q = qbuf[t, mine, :]
+
+            def score(kb, peak):
+                s = lax.dot_general(q, keys(0, kb), (((1,), (1,)), ((), ())), preferred_element_type=F32)
+                sbuf[kb] = s
+                return jnp.maximum(peak, jnp.max(s, axis=1, keepdims=True))
+
+            peak = jnp.full((half, 1), -1e30, F32)
+            if t > 0:
+                peak = lax.fori_loop(0, t, score, peak)
+            s = lax.dot_general(q, keys(0, t), (((1,), (1,)), ((), ())), preferred_element_type=F32)
+            row = lax.broadcasted_iota(jnp.int32, (half, span), 0) + (y * block + part * half)
+            col = lax.broadcasted_iota(jnp.int32, (half, span), 1)
+            s = jnp.where(col <= row, s, -jnp.inf)
+            sbuf[t] = s
+            peak = jnp.maximum(peak, jnp.max(s, axis=1, keepdims=True))
+            place = t * (t + 1) // 2
+
+            def weigh(kb, total):
+                p = jnp.exp2((sbuf[kb] - peak) * factor)
+                probs[place + kb] = p.astype(BF)
+                return total + jnp.sum(p, axis=1, keepdims=True)
+
+            sums.append(lax.fori_loop(0, t + 1, weigh, jnp.zeros((half, 1), F32)))
+        return sums
+
+    def context_rows(part, sums):
+        mine = rows_of(part)
+        for t in range(4):
+            place = t * (t + 1) // 2
+
+            def add(kb, acc):
+                return acc + jnp.dot(probs[place + kb], keys(1, kb), preferred_element_type=F32)
+
+            acc = lax.fori_loop(0, t + 1, add, jnp.zeros((half, HD), F32))
+            cown[t, mine, :] = (acc / sums[t]).astype(BF)
+            itself = jnp.logical_and(z == t, jnp.logical_and(to_y == y, to_c == c))
+
+            @pl.when(jnp.logical_not(itself))
+            def _():
+                direct(
+                    cown.at[t, mine], cx.at[to_c, x, y, mine], ("cd", part), t, y,
+                    z=t, y=to_y, c=to_c,
+                ).start()
+
+            @pl.when(itself)
+            def _():
+                cx[c, x, y, mine, :] = cown[t, mine, :]
+
+    def cx_part(plane, owner, part, h):
+        return cx.at[plane, owner, pl.ds(2 * h, 2), rows_of(part)]
+
+    def cx_pair(owner, label, part, h):
+        mine = cx_part(c, owner, part, h)
+        send(mine, mine, ("cp", label, part, h), c=other)
+
+    def context_around(part):
+        mine = rows_of(part)
+        for source in range(4):
+            itself = jnp.logical_and(source == y, jnp.logical_and(from_z == z, from_c == c))
+
+            @pl.when(jnp.logical_not(itself))
+            def _():
+                ref = cx.at[c, x, source, mine]
+                direct(ref, ref, ("cd", part), source, source, z=z).wait_recv()
+
+        for h, side, where in ((0, "cr", {"x": xr}), (1, "cl", {"x": xl}), (1, "cr", {"x": xr}), (0, "cl", {"x": xl})):
+            send(cx_part(c, x, part, h), cx_part(c, x, part, h), (side, part, h), **where)
+        for h in range(2):
+            cx_pair(x, "own", part, h)
+
+    def context_beside(part):
+        left, right = cx_part(c, xl, part, 0), cx_part(c, xr, part, 1)
+        arrived(left, ("cr", part, 0), x=xr)
+        send(left, left, ("cf", part, 0), x=xr)
+        cx_pair(xl, "left", part, 0)
+        arrived(right, ("cl", part, 1), x=xl)
+        send(right, right, ("cf", part, 1), x=xl)
+        cx_pair(xr, "right", part, 1)
+
+    def context_far(part):
+        arrived(cx_part(c, xl, part, 1), ("cr", part, 1), x=xr)
+        cx_pair(xl, "left", part, 1)
+        arrived(cx_part(c, xr, part, 0), ("cl", part, 0), x=xl)
+        cx_pair(xr, "right", part, 0)
+        arrived(cx_part(c, xf, part, 0), ("cf", part, 0), x=xr)
+        cx_pair(xf, "far", part, 0)
+        arrived(cx_part(c, xf, part, 1), ("cf", part, 1), x=xl)
+        cx_pair(xf, "far", part, 1)
+
+    targets = (yf, yr, yl, y)
+
+    def out_product(part):
+        mine = rows_of(part)
+        for label, owner in (("own", x), ("left", xl), ("right", xr), ("far", xf)):
+            for h in range(2):
+                arrived(cx_part(other, owner, part, h), ("cp", label, part, h), c=other)
+        for i, d in enumerate(targets):
+            for k in range(4):
+                for p in range(2):
+                    lhs[i * half:(i + 1) * half, (2 * k + p) * HD:(2 * k + p + 1) * HD] = cx[p, k, d, mine, :]
+        depth = lhs.shape[1]
+
+        @pl.loop(0, wog.shape[2] // 256)
+        def _(n):
+            cols = pl.ds(pl.multiple_of(n * 256, 256), 256)
+            acc = jnp.dot(lhs[...], wog[:, :, cols].reshape(depth, 256), preferred_element_type=F32)
+            for i in range(3):
+                op[targets[i], mine, cols] = acc[i * half:(i + 1) * half].astype(BF)
+            oacc[mine, cols] = acc[3 * half:]
+
+    quarter = half // 2
+
+    def piece(part, h):
+        return pl.ds(part * half + h * quarter, quarter)
+
+    def out_scatter(part):
+        send(op.at[yf, piece(part, 0)], otr.at[part, 0], ("o", part, "ta"), y=yr)
+        send(op.at[yf, piece(part, 1)], otr.at[part, 1], ("o", part, "tb"), y=yl)
+        send(op.at[yr, piece(part, 1)], ofin.at[0, piece(part, 1)], ("o", part, "a1"), y=yr)
+        send(op.at[yl, piece(part, 0)], ofin.at[1, piece(part, 0)], ("o", part, "b0"), y=yl)
+
+    def out_relay(part):
+        for h, to, where, came, name in ((0, yr, {"y": yr}, "ta", "a0"), (1, yl, {"y": yl}, "tb", "b1")):
+            r = piece(part, h)
+            arrived(otr.at[part, h], ("o", part, came), **where)
+            op[to, r, :] = (op[to, r, :].astype(F32) + otr[part, h].astype(F32)).astype(BF)
+            send(op.at[to, r], ofin.at[h, r], ("o", part, name), **where)
+
+    copies_out = []
+
+    def out_finish(part):
+        arrived(ofin.at[0, piece(part, 1)], ("o", part, "a1"), y=yr)
+        arrived(ofin.at[1, piece(part, 0)], ("o", part, "b0"), y=yl)
+        for h, name, where in ((0, "a0", {"y": yr}), (1, "b1", {"y": yl})):
+            r = piece(part, h)
+            arrived(ofin.at[h, r], ("o", part, name), **where)
+            total = big[x, r, :].astype(F32) + oacc[r, :]
+            lout[r, :] = (total + ofin[0, r, :].astype(F32) + ofin[1, r, :].astype(F32)).astype(BF)
+            copy = pltpu.make_async_copy(lout.at[r], layer_out.at[r], local_sem.at[local_ids("lout", part, h)])
+            copy.start()
+            copies_out.append(copy)
+
+    sums = score_rows(0)
     finish_y(kv_slot(1), "v")
-    for t in range(4):
-        place = t * (t + 1) // 2
-
-        def add(kb, acc):
-            return acc + jnp.dot(probs[place + kb], keys(1, kb), preferred_element_type=F32)
-
-        acc = lax.fori_loop(0, t + 1, add, jnp.zeros((block, HD), F32))
-        cown[t] = (acc / sums[t]).astype(BF)
-        itself = jnp.logical_and(z == t, jnp.logical_and(to_y == y, to_c == c))
-
-        @pl.when(jnp.logical_not(itself))
-        def _():
-            direct(cown.at[t], cx.at[to_c, x, y], "cd", t, y, z=t, y=to_y, c=to_c).start()
-
-        @pl.when(itself)
-        def _():
-            cx[c, x, y] = cown[t]
-
+    context_rows(0, sums)
+    forward("z", out_slot, "wo")
+    context_rows(1, score_rows(1))
+    context_around(0)
     for t in range(4):
         @pl.when(z != t)
         def _():
-            direct(cown.at[t], ctxs.at[z], "c2", t, z, z=t).start()
+            direct(cown.at[t], ctxs.at[z], ("c2",), t, z, z=t).start()
 
         @pl.when(z == t)
         def _():
             ctxs[z] = cown[t]
 
-    forward("z", out_slot, "wo")
-
-    def cx_part(plane, owner, h):
-        return cx.at[plane, owner, pl.ds(2 * h, 2)]
-
-    def cx_pair(owner, label, h):
-        send(cx_part(c, owner, h), cx_part(c, owner, h), ("cp", label, h), c=other)
-
-    for h in range(2):
-        for source in (2 * h, 2 * h + 1):
-            source_z = from_z + c
-            itself = jnp.logical_and(source == y, jnp.logical_and(source_z == z, from_c == c))
-
-            @pl.when(jnp.logical_not(itself))
-            def _():
-                direct(cx.at[c, x, source], cx.at[c, x, source], "cd", source, source, z=z).wait_recv()
-
-        send(cx_part(c, x, h), cx_part(c, x, h), ("cr", h), x=xr)
-        send(cx_part(c, x, h), cx_part(c, x, h), ("cl", h), x=xl)
-        cx_pair(x, "own", h)
-    for t in range(4):
-        itself = jnp.logical_and(z == t, jnp.logical_and(to_y == y, to_c == c))
-
-        @pl.when(jnp.logical_not(itself))
-        def _():
-            direct(cown.at[t], cown.at[t], "cd", t, t, z=z).wait_send()
-
-    arrived(cx_part(c, xl, 0), ("cr", 0), x=xr)
-    send(cx_part(c, xl, 0), cx_part(c, xl, 0), ("cf", 0), x=xr)
-    cx_pair(xl, "left", 0)
-    arrived(cx_part(c, xr, 0), ("cl", 0), x=xl)
-    cx_pair(xr, "right", 0)
-    arrived(cx_part(c, xr, 1), ("cl", 1), x=xl)
-    send(cx_part(c, xr, 1), cx_part(c, xr, 1), ("cf", 1), x=xl)
-    cx_pair(xr, "right", 1)
-    arrived(cx_part(c, xl, 1), ("cr", 1), x=xr)
-    cx_pair(xl, "left", 1)
-
-    context_out = []
+    context_beside(0)
+    context_around(1)
+    context_far(0)
+    finish("z", out_slot, "wo")
+    out_product(0)
+    out_scatter(0)
+    context_beside(1)
+    context_far(1)
+    out_relay(0)
+    out_product(1)
+    out_scatter(1)
+
     for h in range(4):
         @pl.when(z != h)
         def _():
-            copy = direct(ctxs.at[h], ctxs.at[h], "c2", h, h, z=h)
+            copy = direct(ctxs.at[h], ctxs.at[h], ("c2",), h, h, z=h)
             copy.wait_send()
             copy.wait_recv()
 
         copy = pltpu.make_async_copy(
-            ctxs.at[h], ctx_out.at[:, pl.ds(h * HD, HD)], local_sem.at[ids("ctx", h)]
+            ctxs.at[h], ctx_out.at[:, pl.ds(h * HD, HD)], local_sem.at[local_ids("ctx", h)]
         )
         copy.start()
-        context_out.append(copy)
-
-    finish("z", out_slot, "wo")
-    arrived(cx_part(c, xf, 0), ("cf", 0), x=xr)
-    cx_pair(xf, "far", 0)
-    arrived(cx_part(c, xf, 1), ("cf", 1), x=xl)
-    cx_pair(xf, "far", 1)
-    for label, owner in (("own", x), ("left", xl), ("right", xr), ("far", xf)):
-        for h in range(2):
-            arrived(cx_part(other, owner, h), ("cp", label, h), c=other)
-
-    def out_product(d):
-        left = jnp.concatenate([cx[p, k, d] for k in range(4) for p in range(2)], axis=1)
-        right = wog[...].reshape(left.shape[1], wog.shape[2])
-        return jnp.dot(left, right, preferred_element_type=F32)
-
-    def first(ref):
-        return ref.at[pl.ds(0, half)]
-
-    def second(ref):
-        return ref.at[pl.ds(half, half)]
-
-    op[yf] = out_product(yf).astype(BF)
-    send(first(op.at[yf]), otr.at[0], ("o", "ta"), y=yr)
-    send(second(op.at[yf]), otr.at[1], ("o", "tb"), y=yl)
-    op[yr] = out_product(yr).astype(BF)
-    send(second(op.at[yr]), second(ofin.at[0]), ("o", "a1"), y=yr)
-    op[yl] = out_product(yl).astype(BF)
-    send(first(op.at[yl]), first(ofin.at[1]), ("o", "b0"), y=yl)
-    lo, hi = pl.ds(0, half), pl.ds(half, half)
-    arrived(otr.at[0], ("o", "ta"), y=yr)
-    op[yr, lo, :] = (op[yr, lo, :].astype(F32) + otr[0].astype(F32)).astype(BF)
-    send(first(op.at[yr]), first(ofin.at[0]), ("o", "a0"), y=yr)
-    arrived(otr.at[1], ("o", "tb"), y=yl)
-    op[yl, hi, :] = (op[yl, hi, :].astype(F32) + otr[1].astype(F32)).astype(BF)
-    send(second(op.at[yl]), second(ofin.at[1]), ("o", "b1"), y=yl)
-    oacc[...] = big[x].astype(F32) + out_product(y)
-    arrived(second(ofin.at[0]), ("o", "a1"), y=yr)
-    arrived(first(ofin.at[1]), ("o", "b0"), y=yl)
-    out_copies = []
-    for h, side, name, where in ((0, 0, "a0", {"y": yr}), (1, 1, "b1", {"y": yl})):
-        r = pl.ds(h * half, half)
-        arrived(ofin.at[side, r], ("o", name), **where)
-        lout[r, :] = (oacc[r, :] + ofin[0, r, :].astype(F32) + ofin[1, r, :].astype(F32)).astype(BF)
-        copy = pltpu.make_async_copy(lout.at[r], layer_out.at[r], local_sem.at[ids("lout", h)])
-        copy.start()
-        out_copies.append(copy)
+        copies_out.append(copy)
+
+    out_finish(0)
+    out_relay(1)
+    out_finish(1)
+    for t in range(4):
+        itself = jnp.logical_and(z == t, jnp.logical_and(to_y == y, to_c == c))
+
+        @pl.when(jnp.logical_not(itself))
+        def _():
+            for part in range(2):
+                ref = cown.at[t, rows_of(part)]
+                direct(ref, ref, ("cd", part), t, t, z=z).wait_send()
+
     for copy in sends:
         copy.wait_send()
-    for copy in context_out + out_copies:
+    for copy in copies_out:
         copy.wait()
 
 
@@ -602,20 +656,21 @@
             pltpu.VMEM((3, 2, 4 * block, HD), BF),
             pltpu.VMEM((2, 4, 4, block, HD), BF),
             pltpu.VMEM((4, block, HD), BF),
-            pltpu.VMEM((4, block, 4 * block), F32),
-            pltpu.VMEM((10, block, 4 * block), BF),
+            pltpu.VMEM((4, block // 2, 4 * block), F32),
+            pltpu.VMEM((10, block // 2, 4 * block), BF),
             pltpu.VMEM((4, block, HD), BF),
             pltpu.VMEM((2, 4, 4, block, HD), BF),
             pltpu.VMEM((4, block, HD), BF),
             pltpu.VMEM((4, orows, ow), BF),
+            pltpu.VMEM((2 * block, 4 * orows), BF),
             pltpu.VMEM((4, block, ow), BF),
-            pltpu.VMEM((2, block // 2, ow), BF),
+            pltpu.VMEM((2, 2, block // 4, ow), BF),
             pltpu.VMEM((2, block, ow), BF),
             pltpu.VMEM((block, ow), F32),
             pltpu.VMEM((block, ow), BF),
             pltpu.SemaphoreType.DMA((N_MESSAGES,)),
             pltpu.SemaphoreType.DMA((N_MESSAGES,)),
-            pltpu.SemaphoreType.DMA((N_MESSAGES,)),
+            pltpu.SemaphoreType.DMA((N_LOCAL,)),
         ],
         compiler_params=pltpu.CompilerParams(
             collective_id=0, has_side_effects=True, vmem_limit_bytes=62 * 1024 * 1024

time: 137 us -> 132 us (0.964)
  Pallas kernels: 132 us -> 127 us
    pallas_call x1, Pallas kernels: 132 us -> 127 us  [on_device(): pl.pallas_call(body, out_shape=(jax.ShapeDtypeStruct((block, cw), BF), ja...]
where the time goes in v4:
time: 132 us
  Pallas kernels  127 us (96%)
  local copies, waits for them, and re-layouts  3.8 us (3%)
    pallas_call x1, Pallas kernels, on_device(): pl.pallas_call(body, out_shape=(jax.ShapeDtypeStruct((block, cw), BF), ja...  127 us

profile of v4, /device:TPU:1, one launch (start us, length us, event | category | flops | bytes accessed | tf_op | source)
XLA Modules:
  0.0 131.6 jit_solution(10666311022346778517)
XLA Ops:
  0.6 1.3 reshape.7.refs_5_
  1.9 127.2 %shard_map.86 = (bf16[256,512]{1,0:T(8,128)(2,1)}, bf16[256,1024]{1,0:T(8,128)(2,1)}) custom-call(bf16[256,1024]{1,0:T(8,128)(2,1)} %refs_0_.1, bf16[512,512]{1,0:T(8,128)(2,1)} %refs_1_.1, bf16[512,512]{1,0:T(8,128)(2,1)} %refs_2_.1, bf16[512,512]{1,0:T(8,128)(2,1)} %refs_3_.1, bf16[256,1024]{1,0:T(8,128)(2,1)} %refs_4_.1, bf16[1,1024]{1,0:T(2,128)(2,1)} %reshape.7.refs_5_, ...), custom_call_target="tpu_custom_call" | custom-call | tf_op jit(solution)/shard_map/pallas_call | solution.py:637
  129.1 0.0 copy-start
  129.1 1.7 %copy.11 = bf16[256,512]{1,0:T(8,128)(2,1)} copy(bf16[256,512]{1,0:T(8,128)(2,1)} %get-tuple-element.4) | data formatting | bytes 524288
  130.8 0.0 copy-done
  130.8 0.8 copy.12
Async XLA Ops:
  129.1 1.7 %copy-start = (bf16[256,1024]{1,0:T(8,128)(2,1)S(1)}, bf16[256,1024]{1,0:T(8,128)(2,1)}, u32[]{:S(2)}) copy-start(bf16[256,1024]{1,0:T(8,128)(2,1)} %get-tuple-element.5) | copy-start | bytes 1572868

commit v5 on v4

--- a/solution.py
+++ b/solution.py
@@ -32,14 +32,15 @@
         return self.table.setdefault(name, len(self.table))
 
 
-N_MESSAGES = 138
-N_LOCAL = 14
+N_MESSAGES = 132
+N_LOCAL = 17
+N_SENDS = 20
 
 
 def kernel(
-    features, hidden, wq, wk, wv, wout, gain, tables,
+    features, hidden, wq, wk, wv, wout, gain, table_in,
     ctx_out, layer_out,
-    big, transit, gbuf, xs, ssq, sqs, rsc, wg, pbuf, tr, fin, kvg, qbuf, sbuf,
+    big, transit, gbuf, tables, xs, ssq, sqs, rsc, wg, pbuf, tr, fin, kvg, qbuf, sbuf,
     probs, cown, cx, ctxs, wog, lhs, op, otr, ofin, oacc, lout, send_sem, recv_sem, local_sem,
 ):
     z, y, x, c = (lax.axis_index(n) for n in ("z", "y", "x", "c"))
@@ -49,20 +50,48 @@
     other = 1 - c
     block = hidden.shape[0]
     half = block // 2
-    ids, local_ids = Ids(), Ids()
+    ids, local_ids, small = Ids(), Ids(), Ids()
+    unit = big.shape[1] * big.shape[2] // 8
+    groups, classes = (2, 4, 8, 9), {}
     sends = []
+
+    def group_of(src):
+        size = math.prod(src.shape) * src.dtype.itemsize
+        return size // unit if size % unit == 0 else 0
 
     def message(src, dst, name, **where):
         i = ids(*name)
+        g = group_of(src)
+        g = 9 if g == 8 and name[0][0] == "w" else g
+        g = 0 if name[0] == "swap" else g
+        classes[i] = g
+        shared = groups.index(g) if g in groups else len(groups) + small(*name)
         return pltpu.make_async_remote_copy(
-            src_ref=src, dst_ref=dst, send_sem=send_sem.at[i], recv_sem=recv_sem.at[i],
+            src_ref=src, dst_ref=dst, send_sem=send_sem.at[shared], recv_sem=recv_sem.at[i],
             device_id=where, device_id_type=MESH,
         )
 
     def send(src, dst, name, **where):
         copy = message(src, dst, name, **where)
         copy.start()
-        sends.append(copy)
+        sends.append((name, copy))
+
+    def drain():
+        counts = {}
+        for name, copy in sends:
+            g = classes[ids(*name)]
+            if g in groups:
+                counts[g] = counts.get(g, 0) + 1
+            else:
+                copy.wait_send()
+        for g, count in counts.items():
+            lines_out = count * min(g, 8) * unit // (2 * big.shape[2])
+            slots = max(n for n in range(1, 13) if lines_out % (16 * n) == 0 and lines_out // n <= big.shape[1])
+            ref = big.at[pl.ds(0, slots), pl.ds(0, lines_out // slots)]
+            pltpu.make_async_remote_copy(
+                src_ref=ref, dst_ref=ref, send_sem=send_sem.at[groups.index(g)],
+                recv_sem=recv_sem.at[0], device_id={"c": other}, device_id_type=MESH,
+            ).wait_send()
 
     def arrived(dst, name, **where):
         message(dst, dst, name, **where).wait_recv()
@@ -79,18 +108,22 @@
 
     weights = {"k": wk, "v": wv, "q": wq}
     order = {"k": 0, "v": 1, "q": 2}
+    score_factor = math.log2(math.e) / math.sqrt(HD)
     loads = {"x": load(hidden, big.at[x], "x")}
     for name in "kvq":
         loads[name] = load(weights[name], wg.at[order[name], y], name)
-    loads["o"] = load(wout, wog.at[z], "o")
+    loads["o"] = load(wout, wog.at[y], "o")
+    loads["g"] = load(gain, gbuf.at[x, c], "g")
+    loads["t"] = load(table_in, tables, "t")
     pl.semaphore_wait(barrier, len(partners))
 
     lines = {"y": (y, yr, yl, yf), "z": (z, zr, zl, zf)}
 
-    def gather(axis, slot, name):
+    def gather(axis, slot, name, pieces=(0, 1)):
         me, right, left, _ = lines[axis]
-        for h, side, to in ((0, "r", right), (1, "l", left), (1, "r", right), (0, "l", left)):
-            send(slot(me, h), slot(me, h), (name, side, h), **{axis: to})
+        for n in pieces:
+            for h, side, to in ((n, "r", right), (1 - n, "l", left)):
+                send(slot(me, h), slot(me, h), (name, side, h), **{axis: to})
 
     def forward(axis, slot, name):
         _, right, left, _ = lines[axis]
@@ -164,8 +197,10 @@
 
             if k == 0:
                 for label, where in (("zr", {"z": zr}), ("zl", {"z": zl}), ("zz", {"z": zl} if h else {"z": zr})):
-                    sends.append(message(self.part(0, h), self.part(0, h), (self.name, label, h), **where))
-                sends.append(message(self.part(0, h), self.part(0, h), (self.name, "pair", "own", h), c=other))
+                    name = (self.name, label, h)
+                    sends.append((name, message(self.part(0, h), self.part(0, h), name, **where)))
+                name = (self.name, "pair", "own", h)
+                sends.append((name, message(self.part(0, h), self.part(0, h), name, c=other)))
 
         def from_left(self, h):
             mine = self.part(xl, h)
@@ -207,17 +242,17 @@
 
     def process(slot, plane, t, first):
         g = gbuf[z, plane].astype(F32)
-        width = g.shape[1]
+        width = big.shape[2]
 
         @pl.loop(0, block // 32)
         def _(i):
             r = pl.ds(pl.multiple_of(i * 32, 32), 32)
-            v = big[slot, r, :].astype(F32)
-            xs[plane, t, r, :] = (v * g).astype(BF)
-            sq = v * v
-            total = sq[:, :HD]
-            for k in range(1, width // HD):
-                total = total + sq[:, k * HD:(k + 1) * HD]
+            total = None
+            for k in range(width // HD):
+                cols = slice(k * HD, (k + 1) * HD)
+                v = big[slot, r, cols].astype(F32)
+                xs[plane, t, r, cols] = (v * g[k:k + 1, :]).astype(BF)
+                total = v * v if total is None else total + v * v
             if first:
                 ssq[t, r, :] = total
             else:
@@ -231,11 +266,10 @@
     gather_y(weight_slot("k"), "wk")
     loads["v"].wait()
     gather_y(weight_slot("v"), "wv")
-    gain_copy = pltpu.make_async_copy(gain, gbuf.at[x, c], local_sem.at[local_ids("gain")])
-    gain_copy.start()
+    loads["g"].wait()
     gain_sends = [("r", {"x": xr}), ("l", {"x": xl}), ("c", {"c": other})]
     for label, where in gain_sends:
-        send(gain, gbuf.at[x, c], ("gain", label), **where)
+        send(gbuf.at[x, c], gbuf.at[x, c], ("gain", label), **where)
     spread.from_left(0)
     spread.from_right(0)
     spread.from_right(1)
@@ -252,7 +286,6 @@
     send(gbuf.at[xf, c], gbuf.at[xf, c], ("gain", "fc"), c=other)
     spread.pass_on(0)
     spread.pass_on(1)
-    gain_copy.wait()
     arrived(gbuf.at[x, other], ("gain", "c"), c=other)
     arrived(gbuf.at[xl, other], ("gain", "rc"), c=other)
     arrived(gbuf.at[xr, other], ("gain", "lc"), c=other)
@@ -374,6 +407,7 @@
         return ref if part is None else ref.at[pl.ds(part * count, count)]
 
     forward_y(weight_slot("q"), "wq")
+    loads["t"].wait()
     reduced("k")
     for t in range(4):
         kvg[0, t, y] = rotated(total_of("k", t), t).astype(BF)
@@ -389,14 +423,13 @@
     gather_y(kv_slot(1), "v")
     relay("q")
     loads["o"].wait()
-    gather("z", out_slot, "wo")
     forward_y(kv_slot(1), "v")
+    gather("y", out_slot, "wo")
     reduced("q")
     for t in range(4):
-        qbuf[t] = rotated(total_of("q", t), t).astype(BF)
+        qbuf[t] = (rotated(total_of("q", t), t) * score_factor).astype(BF)
     finish_y(kv_slot(0), "k")
 
-    factor = math.log2(math.e) / math.sqrt(HD)
     span = 4 * block
 
     def keys(which, kb):
@@ -407,69 +440,65 @@
 
     def direct(src, dst, name, to, source, **where):
         first = base_of(name)
+        small_base = [small(*name, k) for k in range(4)][0]
         return pltpu.make_async_remote_copy(
-            src_ref=src, dst_ref=dst, send_sem=send_sem.at[first + to],
+            src_ref=src, dst_ref=dst, send_sem=send_sem.at[len(groups) + small_base + to],
             recv_sem=recv_sem.at[first + source], device_id=where, device_id_type=MESH,
         )
 
-    to_y, to_c = 2 * c + z // 2, lax.rem(z, 2)
-    from_z, from_c = 2 * lax.rem(y, 2) + c, y // 2
-
     def rows_of(part):
         return pl.ds(part * half, half)
 
     def score_rows(part):
         mine = rows_of(part)
-        sums = []
         for t in range(4):
             q = qbuf[t, mine, :]
-
-            def score(kb, peak):
+            peak = None
+            for kb in range(t + 1):
                 s = lax.dot_general(q, keys(0, kb), (((1,), (1,)), ((), ())), preferred_element_type=F32)
-                sbuf[kb] = s
-                return jnp.maximum(peak, jnp.max(s, axis=1, keepdims=True))
-
-            peak = jnp.full((half, 1), -1e30, F32)
-            if t > 0:
-                peak = lax.fori_loop(0, t, score, peak)
-            s = lax.dot_general(q, keys(0, t), (((1,), (1,)), ((), ())), preferred_element_type=F32)
-            row = lax.broadcasted_iota(jnp.int32, (half, span), 0) + (y * block + part * half)
-            col = lax.broadcasted_iota(jnp.int32, (half, span), 1)
-            s = jnp.where(col <= row, s, -jnp.inf)
-            sbuf[t] = s
-            peak = jnp.maximum(peak, jnp.max(s, axis=1, keepdims=True))
-            place = t * (t + 1) // 2
-
-            def weigh(kb, total):
-                p = jnp.exp2((sbuf[kb] - peak) * factor)
-                probs[place + kb] = p.astype(BF)
-                return total + jnp.sum(p, axis=1, keepdims=True)
-
-            sums.append(lax.fori_loop(0, t + 1, weigh, jnp.zeros((half, 1), F32)))
-        return sums
-
-    def context_rows(part, sums):
+                if kb == t:
+                    row = lax.broadcasted_iota(jnp.int32, (half, span), 0) + (y * block + part * half)
+                    col = lax.broadcasted_iota(jnp.int32, (half, span), 1)
+                    s = jnp.where(col <= row, s, -jnp.inf)
+                sbuf[t, kb] = s
+                here = jnp.max(s, axis=1, keepdims=True)
+                peak = here if peak is None else jnp.maximum(peak, here)
+            for kb in range(t + 1):
+                cols = slice(kb * span, (kb + 1) * span)
+                probs[t, :, cols] = jnp.exp2(sbuf[t, kb] - peak).astype(BF)
+
+    def context_rows(part):
         mine = rows_of(part)
+        ones = jnp.ones((span, HD), BF)
         for t in range(4):
-            place = t * (t + 1) // 2
-
-            def add(kb, acc):
-                return acc + jnp.dot(probs[place + kb], keys(1, kb), preferred_element_type=F32)
-
-            acc = lax.fori_loop(0, t + 1, add, jnp.zeros((half, HD), F32))
-            cown[t, mine, :] = (acc / sums[t]).astype(BF)
-            itself = jnp.logical_and(z == t, jnp.logical_and(to_y == y, to_c == c))
-
-            @pl.when(jnp.logical_not(itself))
-            def _():
-                direct(
-                    cown.at[t, mine], cx.at[to_c, x, y, mine], ("cd", part), t, y,
-                    z=t, y=to_y, c=to_c,
-                ).start()
-
-            @pl.when(itself)
-            def _():
-                cx[c, x, y, mine, :] = cown[t, mine, :]
+            acc = jnp.zeros((half, 2 * HD), F32)
+            for kb in range(t + 1):
+                right = jnp.concatenate([keys(1, kb), ones], axis=1)
+                cols = slice(kb * span, (kb + 1) * span)
+                acc = acc + jnp.dot(probs[t, :, cols], right, preferred_element_type=F32)
+            cown[t, mine, :] = (acc[:, :HD] / acc[:, HD:]).astype(BF)
+        swap(part, True)
+
+    def swap(part, start):
+        mine = rows_of(part)
+        src, dst = cown.at[:, mine], cx.at[c, z, :, mine]
+        copy = message(src, dst, ("swap", part), z=x, x=z)
+        local = pltpu.make_async_copy(src, cx.at[c, x, :, mine], local_sem.at[local_ids("swap", part)])
+
+        @pl.when(x != z)
+        def _():
+            if start:
+                copy.start()
+            else:
+                copy.wait_recv()
+                copy.wait_send()
+
+        @pl.when(x == z)
+        def _():
+            if start:
+                local.start()
+            else:
+                local.wait()
 
     def cx_part(plane, owner, part, h):
         return cx.at[plane, owner, pl.ds(2 * h, 2), rows_of(part)]
@@ -479,15 +508,7 @@
         send(mine, mine, ("cp", label, part, h), c=other)
 
     def context_around(part):
-        mine = rows_of(part)
-        for source in range(4):
-            itself = jnp.logical_and(source == y, jnp.logical_and(from_z == z, from_c == c))
-
-            @pl.when(jnp.logical_not(itself))
-            def _():
-                ref = cx.at[c, x, source, mine]
-                direct(ref, ref, ("cd", part), source, source, z=z).wait_recv()
-
+        swap(part, False)
         for h, side, where in ((0, "cr", {"x": xr}), (1, "cl", {"x": xl}), (1, "cr", {"x": xr}), (0, "cl", {"x": xl})):
             send(cx_part(c, x, part, h), cx_part(c, x, part, h), (side, part, h), **where)
         for h in range(2):
@@ -512,7 +533,7 @@
         arrived(cx_part(c, xf, part, 1), ("cf", part, 1), x=xl)
         cx_pair(xf, "far", part, 1)
 
-    targets = (yf, yr, yl, y)
+    targets = (zf, zr, zl, z)
 
     def out_product(part):
         mine = rows_of(part)
@@ -522,7 +543,7 @@
         for i, d in enumerate(targets):
             for k in range(4):
                 for p in range(2):
-                    lhs[i * half:(i + 1) * half, (2 * k + p) * HD:(2 * k + p + 1) * HD] = cx[p, k, d, mine, :]
+                    lhs[i * half:(i + 1) * half, (4 * p + k) * HD:(4 * p + k + 1) * HD] = cx[p, k, d, mine, :]
         depth = lhs.shape[1]
 
         @pl.loop(0, wog.shape[2] // 256)
@@ -539,13 +560,13 @@
         return pl.ds(part * half + h * quarter, quarter)
 
     def out_scatter(part):
-        send(op.at[yf, piece(part, 0)], otr.at[part, 0], ("o", part, "ta"), y=yr)
-        send(op.at[yf, piece(part, 1)], otr.at[part, 1], ("o", part, "tb"), y=yl)
-        send(op.at[yr, piece(part, 1)], ofin.at[0, piece(part, 1)], ("o", part, "a1"), y=yr)
-        send(op.at[yl, piece(part, 0)], ofin.at[1, piece(part, 0)], ("o", part, "b0"), y=yl)
+        send(op.at[zf, piece(part, 0)], otr.at[part, 0], ("o", part, "ta"), z=zr)
+        send(op.at[zf, piece(part, 1)], otr.at[part, 1], ("o", part, "tb"), z=zl)
+        send(op.at[zr, piece(part, 1)], ofin.at[0, piece(part, 1)], ("o", part, "a1"), z=zr)
+        send(op.at[zl, piece(part, 0)], ofin.at[1, piece(part, 0)], ("o", part, "b0"), z=zl)
 
     def out_relay(part):
-        for h, to, where, came, name in ((0, yr, {"y": yr}, "ta", "a0"), (1, yl, {"y": yl}, "tb", "b1")):
+        for h, to, where, came, name in ((0, zr, {"z": zr}, "ta", "a0"), (1, zl, {"z": zl}, "tb", "b1")):
             r = piece(part, h)
             arrived(otr.at[part, h], ("o", part, came), **where)
             op[to, r, :] = (op[to, r, :].astype(F32) + otr[part, h].astype(F32)).astype(BF)
@@ -554,9 +575,9 @@
     copies_out = []
 
     def out_finish(part):
-        arrived(ofin.at[0, piece(part, 1)], ("o", part, "a1"), y=yr)
-        arrived(ofin.at[1, piece(part, 0)], ("o", part, "b0"), y=yl)
-        for h, name, where in ((0, "a0", {"y": yr}), (1, "b1", {"y": yl})):
+        arrived(ofin.at[0, piece(part, 1)], ("o", part, "a1"), z=zr)
+        arrived(ofin.at[1, piece(part, 0)], ("o", part, "b0"), z=zl)
+        for h, name, where in ((0, "a0", {"z": zr}), (1, "b1", {"z": zl})):
             r = piece(part, h)
             arrived(ofin.at[h, r], ("o", part, name), **where)
             total = big[x, r, :].astype(F32) + oacc[r, :]
@@ -565,11 +586,12 @@
             copy.start()
             copies_out.append(copy)
 
-    sums = score_rows(0)
+    score_rows(0)
     finish_y(kv_slot(1), "v")
-    context_rows(0, sums)
-    forward("z", out_slot, "wo")
-    context_rows(1, score_rows(1))
+    context_rows(0)
+    score_rows(1)
+    forward("y", out_slot, "wo")
+    context_rows(1)
     context_around(0)
     for t in range(4):
         @pl.when(z != t)
@@ -583,10 +605,10 @@
     context_beside(0)
     context_around(1)
     context_far(0)
-    finish("z", out_slot, "wo")
+    context_beside(1)
+    finish("y", out_slot, "wo")
     out_product(0)
     out_scatter(0)
-    context_beside(1)
     context_far(1)
     out_relay(0)
     out_product(1)
@@ -608,17 +630,7 @@
     out_finish(0)
     out_relay(1)
     out_finish(1)
-    for t in range(4):
-        itself = jnp.logical_and(z == t, jnp.logical_and(to_y == y, to_c == c))
-
-        @pl.when(jnp.logical_not(itself))
-        def _():
-            for part in range(2):
-                ref = cown.at[t, rows_of(part)]
-                direct(ref, ref, ("cd", part), t, t, z=z).wait_send()
-
-    for copy in sends:
-        copy.wait_send()
+    drain()
     for copy in copies_out:
         copy.wait()
 
@@ -629,7 +641,6 @@
     orows, ow = w_out.shape
     features = 8 * width
     tables = jnp.asarray(rotary_tables(block, 16))
-    vmem = pl.BlockSpec(memory_space=pltpu.VMEM)
 
     def body(*refs):
         kernel(features, *refs)
@@ -640,12 +651,13 @@
             jax.ShapeDtypeStruct((block, cw), BF),
             jax.ShapeDtypeStruct((block, ow), BF),
         ),
-        in_specs=[pl.BlockSpec(memory_space=pl.ANY)] * 5 + [vmem] * 2,
+        in_specs=[pl.BlockSpec(memory_space=pl.ANY)] * 7,
         out_specs=(pl.BlockSpec(memory_space=pl.ANY),) * 2,
         scratch_shapes=[
             pltpu.VMEM((12, block, width), BF),
             pltpu.VMEM((2, block // 2, width), BF),
-            pltpu.VMEM((4, 2, 1, width), BF),
+            pltpu.VMEM((4, 2, width // HD, HD), BF),
+            pltpu.VMEM((16 + block, 2 * HD), F32),
             pltpu.VMEM((2, 4, block, width), BF),
             pltpu.VMEM((4, block, HD), F32),
             pltpu.VMEM((4, 4, 8, block), F32),
@@ -656,8 +668,8 @@
             pltpu.VMEM((3, 2, 4 * block, HD), BF),
             pltpu.VMEM((2, 4, 4, block, HD), BF),
             pltpu.VMEM((4, block, HD), BF),
-            pltpu.VMEM((4, block // 2, 4 * block), F32),
-            pltpu.VMEM((10, block // 2, 4 * block), BF),
+            pltpu.VMEM((4, 4, block // 2, 4 * block), F32),
+            pltpu.VMEM((4, block // 2, 16 * block), BF),
             pltpu.VMEM((4, block, HD), BF),
             pltpu.VMEM((2, 4, 4, block, HD), BF),
             pltpu.VMEM((4, block, HD), BF),
@@ -668,14 +680,14 @@
             pltpu.VMEM((2, block, ow), BF),
             pltpu.VMEM((block, ow), F32),
             pltpu.VMEM((block, ow), BF),
-            pltpu.SemaphoreType.DMA((N_MESSAGES,)),
+            pltpu.SemaphoreType.DMA((N_SENDS,)),
             pltpu.SemaphoreType.DMA((N_MESSAGES,)),
             pltpu.SemaphoreType.DMA((N_LOCAL,)),
         ],
         compiler_params=pltpu.CompilerParams(
             collective_id=0, has_side_effects=True, vmem_limit_bytes=62 * 1024 * 1024
         ),
-    )(hidden, w_query, w_key, w_value, w_out, norm_gain.reshape(1, width), tables)
+    )(hidden, w_query, w_key, w_value, w_out, norm_gain.reshape(width // HD, HD), tables)
 
 
 def solution(mesh):

time: 132 us -> 126 us (0.955)
  Pallas kernels: 127 us -> 122 us
    pallas_call x1, Pallas kernels: 127 us -> 122 us  [on_device(): pl.pallas_call(body, out_shape=(jax.ShapeDtypeStruct((block, cw), BF), ja...]
where the time goes in v5:
time: 126 us; the launch traced here: 125 us
  Pallas kernels  122 us (97%)
  local copies, waits for them, and re-layouts  2.52 us (2%)
    pallas_call x1, Pallas kernels, on_device(): pl.pallas_call(body, out_shape=(jax.ShapeDtypeStruct((block, cw), BF), ja...  122 us
    unnamed x4, local copies, waits for them, and re-layouts  2.52 us

profile of v5, /device:TPU:1, one launch (start us, length us, event | category | flops | bytes accessed | tf_op | source)
XLA Modules:
  0.0 125.5 jit_solution(9077394023944373982)
XLA Ops:
  0.6 122.3 %shard_map.86 = (bf16[256,512]{1,0:T(8,128)(2,1)}, bf16[256,1024]{1,0:T(8,128)(2,1)}) custom-call(bf16[256,1024]{1,0:T(8,128)(2,1)} %refs_0_.1, bf16[512,512]{1,0:T(8,128)(2,1)} %refs_1_.1, bf16[512,512]{1,0:T(8,128)(2,1)} %refs_2_.1, bf16[512,512]{1,0:T(8,128)(2,1)} %refs_3_.1, bf16[256,1024]{1,0:T(8,128)(2,1)} %refs_4_.1, bf16[8,128]{1,0:T(8,128)(2,1)} %bitcast.1, ...), custom_call_target="tpu_custom_call" | custom-call | tf_op jit(solution)/shard_map/pallas_call | solution.py:648
  122.9 0.0 copy-start
  122.9 1.7 %copy.11 = bf16[256,512]{1,0:T(8,128)(2,1)} copy(bf16[256,512]{1,0:T(8,128)(2,1)} %get-tuple-element.4) | data formatting | bytes 524288
  124.7 0.0 copy-done
  124.7 0.8 copy.12
Async XLA Ops:
  122.9 1.7 %copy-start = (bf16[256,1024]{1,0:T(8,128)(2,1)S(1)}, bf16[256,1024]{1,0:T(8,128)(2,1)}, u32[]{:S(2)}) copy-start(bf16[256,1024]{1,0:T(8,128)(2,1)} %get-tuple-element.5) | copy-start | bytes 1572868

commit v6 on v5

--- a/solution.py
+++ b/solution.py
@@ -33,7 +33,7 @@
 
 
 N_MESSAGES = 132
-N_LOCAL = 17
+N_LOCAL = 9
 N_SENDS = 20
 
 
@@ -41,7 +41,7 @@
     features, hidden, wq, wk, wv, wout, gain, table_in,
     ctx_out, layer_out,
     big, transit, gbuf, tables, xs, ssq, sqs, rsc, wg, pbuf, tr, fin, kvg, qbuf, sbuf,
-    probs, cown, cx, ctxs, wog, lhs, op, otr, ofin, oacc, lout, send_sem, recv_sem, local_sem,
+    probs, cown, cx, ctxs, wog, lhs, op, otr, ofin, oacc, send_sem, recv_sem, local_sem,
 ):
     z, y, x, c = (lax.axis_index(n) for n in ("z", "y", "x", "c"))
     zr, zl, zf = (lax.rem(z + k, 4) for k in (1, 3, 2))
@@ -164,11 +164,12 @@
         def part(self, slot, h):
             return self.buf.at[slot, pl.ds(h * self.rows, self.rows)]
 
-        def own(self, h):
-            mine = self.part(x, h)
-            send(mine, mine, (self.name, "xr", h), x=xr)
-            send(mine, mine, (self.name, "xl", h), x=xl)
-            self.onward(0, h)
+        def own(self):
+            for h, side, to in ((0, "xr", xr), (1, "xl", xl), (1, "xr", xr), (0, "xl", xl)):
+                mine = self.part(x, h)
+                send(mine, mine, (self.name, side, h), x=to)
+            self.onward(0, 0)
+            self.onward(0, 1)
 
         def pair(self, src_slot, owner, label, h):
             send(self.part(src_slot, h), self.part(8 + owner, h), (self.name, "pair", label, h), c=other)
@@ -260,8 +261,7 @@
 
     spread = Spread("h", big, transit)
     loads["x"].wait()
-    for h in range(2):
-        spread.own(h)
+    spread.own()
     loads["k"].wait()
     gather_y(weight_slot("k"), "wk")
     loads["v"].wait()
@@ -271,8 +271,8 @@
     for label, where in gain_sends:
         send(gbuf.at[x, c], gbuf.at[x, c], ("gain", label), **where)
     spread.from_left(0)
+    spread.from_right(1)
     spread.from_right(0)
-    spread.from_right(1)
     spread.from_left(1)
     arrived(gbuf.at[xl, c], ("gain", "r"), x=xr)
     send(gbuf.at[xl, c], gbuf.at[xl, c], ("gain", "rf"), x=xr)
@@ -540,28 +540,44 @@
         for label, owner in (("own", x), ("left", xl), ("right", xr), ("far", xf)):
             for h in range(2):
                 arrived(cx_part(other, owner, part, h), ("cp", label, part, h), c=other)
-        for i, d in enumerate(targets):
-            for k in range(4):
-                for p in range(2):
-                    lhs[i * half:(i + 1) * half, (4 * p + k) * HD:(4 * p + k + 1) * HD] = cx[p, k, d, mine, :]
         depth = lhs.shape[1]
 
-        @pl.loop(0, wog.shape[2] // 256)
-        def _(n):
-            cols = pl.ds(pl.multiple_of(n * 256, 256), 256)
-            acc = jnp.dot(lhs[...], wog[:, :, cols].reshape(depth, 256), preferred_element_type=F32)
-            for i in range(3):
-                op[targets[i], mine, cols] = acc[i * half:(i + 1) * half].astype(BF)
-            oacc[mine, cols] = acc[3 * half:]
+        def product(first_target, count):
+            for i in range(first_target, first_target + count):
+                for k in range(4):
+                    for p in range(2):
+                        lhs[i * half:(i + 1) * half, (4 * p + k) * HD:(4 * p + k + 1) * HD] = cx[p, k, targets[i], mine, :]
+
+            @pl.loop(0, wog.shape[2] // 256)
+            def _(n):
+                cols = pl.ds(pl.multiple_of(n * 256, 256), 256)
+                left = lhs[first_target * half:(first_target + count) * half, :]
+                acc = jnp.dot(left, wog[:, :, cols].reshape(depth, 256), preferred_element_type=F32)
+                for i in range(first_target, first_target + count):
+                    rows = slice((i - first_target) * half, (i - first_target + 1) * half)
+                    if i < 3:
+                        op[targets[i], mine, cols] = acc[rows].astype(BF)
+                    else:
+                        oacc[mine, cols] = acc[rows]
+
+        if part == 0:
+            product(0, 1)
+            out_across(part)
+            product(1, 3)
+            out_scatter(part)
+        else:
+            product(0, 4)
 
     quarter = half // 2
 
     def piece(part, h):
         return pl.ds(part * half + h * quarter, quarter)
 
-    def out_scatter(part):
+    def out_across(part):
         send(op.at[zf, piece(part, 0)], otr.at[part, 0], ("o", part, "ta"), z=zr)
         send(op.at[zf, piece(part, 1)], otr.at[part, 1], ("o", part, "tb"), z=zl)
+
+    def out_scatter(part):
         send(op.at[zr, piece(part, 1)], ofin.at[0, piece(part, 1)], ("o", part, "a1"), z=zr)
         send(op.at[zl, piece(part, 0)], ofin.at[1, piece(part, 0)], ("o", part, "b0"), z=zl)
 
@@ -571,8 +587,6 @@
             arrived(otr.at[part, h], ("o", part, came), **where)
             op[to, r, :] = (op[to, r, :].astype(F32) + otr[part, h].astype(F32)).astype(BF)
             send(op.at[to, r], ofin.at[h, r], ("o", part, name), **where)
-
-    copies_out = []
 
     def out_finish(part):
         arrived(ofin.at[0, piece(part, 1)], ("o", part, "a1"), z=zr)
@@ -581,10 +595,7 @@
             r = piece(part, h)
             arrived(ofin.at[h, r], ("o", part, name), **where)
             total = big[x, r, :].astype(F32) + oacc[r, :]
-            lout[r, :] = (total + ofin[0, r, :].astype(F32) + ofin[1, r, :].astype(F32)).astype(BF)
-            copy = pltpu.make_async_copy(lout.at[r], layer_out.at[r], local_sem.at[local_ids("lout", part, h)])
-            copy.start()
-            copies_out.append(copy)
+            layer_out[r, :] = (total + ofin[0, r, :].astype(F32) + ofin[1, r, :].astype(F32)).astype(BF)
 
     score_rows(0)
     finish_y(kv_slot(1), "v")
@@ -605,13 +616,13 @@
     context_beside(0)
     context_around(1)
     context_far(0)
-    context_beside(1)
     finish("y", out_slot, "wo")
     out_product(0)
-    out_scatter(0)
+    context_beside(1)
     context_far(1)
     out_relay(0)
     out_product(1)
+    out_across(1)
     out_scatter(1)
 
     for h in range(4):
@@ -621,18 +632,12 @@
             copy.wait_send()
             copy.wait_recv()
 
-        copy = pltpu.make_async_copy(
-            ctxs.at[h], ctx_out.at[:, pl.ds(h * HD, HD)], local_sem.at[local_ids("ctx", h)]
-        )
-        copy.start()
-        copies_out.append(copy)
+        ctx_out[:, h * HD:(h + 1) * HD] = ctxs[h]
 
     out_finish(0)
     out_relay(1)
     out_finish(1)
     drain()
-    for copy in copies_out:
-        copy.wait()
 
 
 def on_device(hidden, norm_gain, w_query, w_key, w_value, w_out):
@@ -648,11 +653,11 @@
     return pl.pallas_call(
         body,
         out_shape=(
-            jax.ShapeDtypeStruct((block, cw), BF),
-            jax.ShapeDtypeStruct((block, ow), BF),
+            pltpu.VMEM((block, cw), BF),
+            pltpu.VMEM((block, ow), BF),
         ),
         in_specs=[pl.BlockSpec(memory_space=pl.ANY)] * 7,
-        out_specs=(pl.BlockSpec(memory_space=pl.ANY),) * 2,
+        out_specs=(pl.BlockSpec(memory_space=pltpu.VMEM),) * 2,
         scratch_shapes=[
             pltpu.VMEM((12, block, width), BF),
             pltpu.VMEM((2, block // 2, width), BF),
@@ -679,7 +684,6 @@
             pltpu.VMEM((2, 2, block // 4, ow), BF),
             pltpu.VMEM((2, block, ow), BF),
             pltpu.VMEM((block, ow), F32),
-            pltpu.VMEM((block, ow), BF),
             pltpu.SemaphoreType.DMA((N_SENDS,)),
             pltpu.SemaphoreType.DMA((N_MESSAGES,)),
             pltpu.SemaphoreType.DMA((N_LOCAL,)),

time: 126 us -> 124 us (0.984)
    unnamed x4 -> x2, local copies, waits for them, and re-layouts: 2.52 us -> 1.5 us
where the time goes in v6:
time: 124 us
  Pallas kernels  122 us (98%)
  local copies, waits for them, and re-layouts  1.5 us (1%)
    pallas_call x1, Pallas kernels, on_device(): pl.pallas_call(body, out_shape=(pltpu.VMEM((block, cw), BF), pltpu.VMEM((...  122 us

profile of v6, /device:TPU:1, one launch (start us, length us, event | category | flops | bytes accessed | tf_op | source)
XLA Modules:
  0.0 124.3 jit_solution(13930316726911569295)
XLA Ops:
  0.6 122.2 %shard_map.86 = (bf16[256,512]{1,0:T(8,128)(2,1)S(1)}, bf16[256,1024]{1,0:T(8,128)(2,1)S(1)}) custom-call(bf16[256,1024]{1,0:T(8,128)(2,1)} %refs_0_.1, bf16[512,512]{1,0:T(8,128)(2,1)} %refs_1_.1, bf16[512,512]{1,0:T(8,128)(2,1)} %refs_2_.1, bf16[512,512]{1,0:T(8,128)(2,1)} %refs_3_.1, bf16[256,1024]{1,0:T(8,128)(2,1)} %refs_4_.1, bf16[8,128]{1,0:T(8,128)(2,1)} %bitcast.1, ...), custom_call_target="tpu_custom_call" | custom-call | tf_op jit(solution)/shard_map/pallas_call | solution.py:653
  122.8 0.7 copy.11
  123.5 0.8 copy.12

commit v7 on v6

--- a/solution.py
+++ b/solution.py
@@ -32,7 +32,7 @@
         return self.table.setdefault(name, len(self.table))
 
 
-N_MESSAGES = 132
+N_MESSAGES = 91
 N_LOCAL = 9
 N_SENDS = 20
 
@@ -53,14 +53,25 @@
     ids, local_ids, small = Ids(), Ids(), Ids()
     unit = big.shape[1] * big.shape[2] // 8
     groups, classes = (2, 4, 8, 9), {}
+    gathered = ("wk", "wv", "wq", "k", "v", "wo")
+    order = {"k": 0, "v": 1, "q": 2}
     sends = []
 
     def group_of(src):
         size = math.prod(src.shape) * src.dtype.itemsize
         return size // unit if size % unit == 0 else 0
 
+    def arrival(name):
+        if name[0] in gathered and name[1:] in (("r", 1), ("l", 0), ("fr",), ("fl",)):
+            return name[0], "rest"
+        if name[0] in order and name[1] in ("a0", "a1", "b0", "b1"):
+            return name[0], "sum"
+        if name[0] == "cp":
+            return "cp", name[2]
+        return name
+
     def message(src, dst, name, **where):
-        i = ids(*name)
+        i = ids(*arrival(name))
         g = group_of(src)
         g = 9 if g == 8 and name[0][0] == "w" else g
         g = 0 if name[0] == "swap" else g
@@ -79,7 +90,7 @@
     def drain():
         counts = {}
         for name, copy in sends:
-            g = classes[ids(*name)]
+            g = classes[ids(*arrival(name))]
             if g in groups:
                 counts[g] = counts.get(g, 0) + 1
             else:
@@ -94,7 +105,10 @@
             ).wait_send()
 
     def arrived(dst, name, **where):
-        message(dst, dst, name, **where).wait_recv()
+        pltpu.make_async_remote_copy(
+            src_ref=dst, dst_ref=dst, send_sem=send_sem.at[0], recv_sem=recv_sem.at[ids(*arrival(name))],
+            device_id=where, device_id_type=MESH,
+        ).wait_recv()
 
     barrier = pltpu.get_barrier_semaphore()
     partners = [{"z": zr}, {"z": zl}, {"z": zf}, {"y": yr}, {"y": yl}, {"x": xr}, {"x": xl}, {"c": other}]
@@ -133,11 +147,11 @@
         send(slot(right, 1), slot(right, 1), (name, "fl"), **{axis: left})
 
     def finish(axis, slot, name):
-        _, right, left, far = lines[axis]
-        arrived(slot(left, 1), (name, "r", 1), **{axis: right})
-        arrived(slot(right, 0), (name, "l", 0), **{axis: left})
-        arrived(slot(far, 0), (name, "fr"), **{axis: right})
-        arrived(slot(far, 1), (name, "fl"), **{axis: left})
+        if name in ("k", "v"):
+            rest = kvg.at[0 if name == "k" else 1, :, pl.ds(0, 2)]
+        else:
+            rest = wog.at[pl.ds(0, 2)] if name == "wo" else wg.at[order[name[1]], pl.ds(0, 2)]
+        arrived(rest, (name, "rest"), c=other)
 
     def gather_y(slot, name):
         gather("y", slot, name)
@@ -356,10 +370,7 @@
 
     def reduced(name):
         j = order[name]
-        arrived(upper(fin.at[j, 0]), (name, "a1"), z=zr)
-        arrived(lower(fin.at[j, 1]), (name, "b0"), z=zl)
-        arrived(lower(fin.at[j, 0]), (name, "a0"), z=zr)
-        arrived(upper(fin.at[j, 1]), (name, "b1"), z=zl)
+        arrived(fin.at[j], (name, "sum"), c=other)
 
     def total_of(name, t):
         j = order[name]
@@ -537,9 +548,7 @@
 
     def out_product(part):
         mine = rows_of(part)
-        for label, owner in (("own", x), ("left", xl), ("right", xr), ("far", xf)):
-            for h in range(2):
-                arrived(cx_part(other, owner, part, h), ("cp", label, part, h), c=other)
+        arrived(cx.at[other, :, :, mine], ("cp", "any", part), c=other)
         depth = lhs.shape[1]
 
         def product(first_target, count):

time: 124 us -> 124 us (level)
  no operation moved by 1% of the time
where the time goes in v7:
time: 124 us
  Pallas kernels  122 us (98%)
  local copies, waits for them, and re-layouts  1.5 us (1%)
    pallas_call x1, Pallas kernels, on_device(): pl.pallas_call(body, out_shape=(pltpu.VMEM((block, cw), BF), pltpu.VMEM((...  122 us

profile of v7, /device:TPU:1, one launch (start us, length us, event | category | flops | bytes accessed | tf_op | source)
XLA Modules:
  0.0 124.0 jit_solution(14750862492799931113)
XLA Ops:
  0.6 121.8 %shard_map.86 = (bf16[256,512]{1,0:T(8,128)(2,1)S(1)}, bf16[256,1024]{1,0:T(8,128)(2,1)S(1)}) custom-call(bf16[256,1024]{1,0:T(8,128)(2,1)} %refs_0_.1, bf16[512,512]{1,0:T(8,128)(2,1)} %refs_1_.1, bf16[512,512]{1,0:T(8,128)(2,1)} %refs_2_.1, bf16[512,512]{1,0:T(8,128)(2,1)} %refs_3_.1, bf16[256,1024]{1,0:T(8,128)(2,1)} %refs_4_.1, bf16[8,128]{1,0:T(8,128)(2,1)} %bitcast.1, ...), custom_call_target="tpu_custom_call" | custom-call | tf_op jit(solution)/shard_map/pallas_call | solution.py:662
  122.5 0.7 copy.11
  123.2 0.8 copy.12
